TPU v7x, 128 devices: a whole 4x4x4 slice. The times are simulated.
128 devices in a mesh: ctx: 32 (over z, x, core), exp: 4 (over y).
Axes of the slice: x: 4, y: 4, z: 4, core: 2. Of those that a mesh axis runs over, the one named last changes fastest.
Arguments:
- queries: bfloat16 [8192, 4096], P('ctx', 'exp'), may hold values from -6 to 6
- key_rows: bfloat16 [8192, 4096], P('ctx', 'exp'), may hold values from -6 to 6
- value_rows: bfloat16 [8192, 4096], P('ctx', 'exp'), may hold values from -6 to 6
- gate_rows: bfloat16 [8192, 4096], P('ctx', 'exp'), may hold values from -6 to 6
- decay_exp: int32 [32], P('exp'), may hold values from 5 to 16
- attn_gain: float32 [4096], P('exp'), may hold values from 0.1 to 1.9
- out_proj: bfloat16 [4096, 6144], P('exp'), may hold values from -0.09375 to 0.09375
- residual: bfloat16 [8192, 6144], P(('ctx', 'exp')), may hold values from -6 to 6
- norm_gain: float32 [6144], replicated, may hold values from 0.1 to 1.9
- routes: int32 [8192, 2], P('ctx'), may hold values from 0 to 31, as said below
- route_weights: float32 [8192, 2], P('ctx'), may hold values from 0.1 to 1
- w_gate: bfloat16 [4, 9216, 6144], P('exp', 'ctx'), may hold values from -0.078125 to 0.078125
- w_up: bfloat16 [4, 9216, 6144], P('exp', 'ctx'), may hold values from -0.078125 to 0.078125
- w_down: bfloat16 [4, 9216, 6144], P('exp', 'ctx'), may hold values from -0.0625 to 0.0625
Outputs:
- layer_out: bfloat16 [8192, 6144], P(('ctx', 'exp'))
Inputs may be any that keep to these rules, and one draw needn't show every extreme that they name: `routes`: A row's two entries differ. An expert e below 4 is named only in column e % 2. In every aligned block of 64 rows each expert below 4 is named at most 8 times, and some expert below 4 exactly 8 times.
All inputs are finite; a program needn't handle non-finite values.
Results may differ from a plain program's by a relative error of at most 0.018.
Values may be sent and summed in bfloat16 or wider, within the bound.
A program may use at most 128 MiB of HBM per device.

v0:
```python
import jax
import jax.numpy as jnp
from jax import lax
from jax.sharding import PartitionSpec as P

EPSILON = 1e-06


def prefix(shard, axis, combine, identity):
    size, index = (lax.axis_size(axis), lax.axis_index(axis))
    everything = jax.tree.map(
        lambda part, kind: lax.all_gather(part.astype(kind), axis),
        shard,
        (jnp.bfloat16, jnp.bfloat16),
    )
    start = jax.tree.map(
        lambda part, zero: jnp.broadcast_to(jnp.asarray(zero, part.dtype), part.shape),
        shard,
        identity,
    )

    def turn(k, before):
        reached = k < index
        new = combine(
            before, jax.tree.map(lambda part, own: part[k].astype(own.dtype), everything, shard)
        )
        return jax.tree.map(lambda a, b: jnp.where(reached, a, b), new, before)

    return lax.fori_loop(0, size, turn, start)


def span_local(queries, key_rows, value_rows, decay_exp):
    row_count = queries.shape[0]
    head_count = decay_exp.shape[0]
    head_width = queries.shape[1] // head_count
    query_heads = queries.reshape(row_count, head_count, head_width)
    key_heads = key_rows.reshape(row_count, head_count, head_width)
    value_heads = value_rows.reshape(row_count, head_count, head_width)
    decay_rates = jnp.exp2(-decay_exp.astype(jnp.float32))
    positions = jnp.arange(row_count, dtype=jnp.float32)
    offsets = positions[:, None] - positions[None, :]
    damping = jnp.where(
        offsets[None] >= 0.0,
        jnp.exp(-decay_rates[:, None, None] * jnp.maximum(offsets, 0.0)[None]),
        0.0,
    )
    scores = jnp.einsum("thd,shd->hts", query_heads, key_heads, preferred_element_type=jnp.float32)
    mixing = (scores * damping).astype(jnp.bfloat16)
    inner_part = jnp.einsum("hts,shd->thd", mixing, value_heads, preferred_element_type=jnp.float32)
    tail_decay = jnp.exp(-decay_rates[None, :] * (row_count - 1.0 - positions)[:, None])
    keyed_rows = (key_heads.astype(jnp.float32) * tail_decay[:, :, None]).astype(jnp.bfloat16)
    update = jnp.einsum("shd,she->hde", keyed_rows, value_heads, preferred_element_type=jnp.float32)
    carry_decay = jnp.exp(-decay_rates * row_count)
    lead_decay = jnp.exp(-decay_rates[None, :] * (positions + 1.0)[:, None])
    leading = query_heads.astype(jnp.float32) * lead_decay[:, :, None]
    return (inner_part, leading, update, carry_decay)


def join_states(earlier, later):
    return (earlier[0] * later[0], later[0][:, None, None] * earlier[1] + later[1])


def settle(inner_part, leading, prior_state, gate_rows, attn_gain):
    outer_part = jnp.einsum("thd,hde->the", leading, prior_state, precision=lax.Precision.HIGHEST)
    mixed_heads = inner_part + outer_part
    row_count, head_count, head_width = mixed_heads.shape
    mean_square = jnp.mean(mixed_heads * mixed_heads, axis=2, keepdims=True)
    normed_heads = mixed_heads * lax.rsqrt(mean_square + EPSILON)
    gain_heads = attn_gain.reshape(head_count, head_width)
    gate_heads = gate_rows.reshape(row_count, head_count, head_width).astype(jnp.float32)
    settled = (normed_heads * gain_heads * jax.nn.sigmoid(gate_heads)).astype(jnp.bfloat16)
    return settled.reshape(row_count, head_count * head_width)


def token_norm(hidden, norm_gain):
    mean_square = jnp.mean(hidden * hidden, axis=1, keepdims=True)
    return (hidden * lax.rsqrt(mean_square + EPSILON) * norm_gain).astype(jnp.bfloat16)


def slot_tables(owners, chosen_ids, weights, capacity):
    column = owners % 2
    chosen = jnp.where(column[:, None] == 0, chosen_ids[None, :, 0], chosen_ids[None, :, 1])
    weight_rows = jnp.where(column[:, None] == 0, weights[None, :, 0], weights[None, :, 1])
    picked = chosen == owners[:, None]
    slot_rank = jnp.cumsum(picked.astype(jnp.int32), axis=1) - 1
    slot_ids = jnp.arange(capacity, dtype=jnp.int32)
    slot_table = picked[:, None, :] & (slot_rank[:, None, :] == slot_ids[None, :, None])
    return (slot_table.astype(jnp.bfloat16), jnp.where(slot_table, weight_rows[:, None, :], 0.0))


def expert_part(slot_rows, gate_cols, up_cols, down_rows):
    contract_dims = (((1,), (1,)), ((), ()))
    first_half = lax.dot_general(
        slot_rows, gate_cols, contract_dims, preferred_element_type=jnp.float32
    )
    second_half = lax.dot_general(
        slot_rows, up_cols, contract_dims, preferred_element_type=jnp.float32
    )
    activated = (jax.nn.silu(first_half) * second_half).astype(jnp.bfloat16)
    return jnp.dot(activated, down_rows, preferred_element_type=jnp.float32)


def body(
    queries,
    key_rows,
    value_rows,
    gate_rows,
    decay_exp,
    attn_gain,
    out_proj,
    residual,
    norm_gain,
    routes,
    route_weights,
    w_gate,
    w_up,
    w_down,
):
    inner_part, leading, update, carry_decay = span_local(queries, key_rows, value_rows, decay_exp)
    head_count = decay_exp.shape[0]
    head_width = queries.shape[1] // head_count
    identity = (
        jnp.ones((head_count,), jnp.float32),
        jnp.zeros((head_count, head_width, head_width), jnp.float32),
    )
    carried, prior_state = prefix((carry_decay, update), "ctx", join_states, identity)
    settled = settle(inner_part, leading, prior_state, gate_rows, attn_gain)
    span_rows = queries.shape[0]
    group_count = lax.axis_size("exp")
    group_rows = span_rows // group_count
    group_index = lax.axis_index("exp")
    first_mine = group_index * group_rows
    capacity = group_rows // 8
    gate_cols = w_gate[0]
    up_cols = w_up[0]
    down_rows = w_down[0]
    placed = lax.dynamic_update_slice_in_dim(
        jnp.zeros((span_rows, residual.shape[1]), jnp.float32),
        residual.astype(jnp.float32),
        first_mine,
        0,
    )
    projected = jnp.dot(settled, out_proj, preferred_element_type=jnp.float32) + placed
    hidden_all = lax.psum(projected.astype(jnp.bfloat16), "exp").astype(jnp.float32)
    normed_all = token_norm(hidden_all, norm_gain)
    owners = jnp.reshape(group_index, (1,))
    slot_table, weighted = slot_tables(owners, routes, route_weights, capacity * group_count)
    outgoing = jnp.einsum(
        "ecn,nd->cd", slot_table, normed_all, preferred_element_type=jnp.float32
    ).astype(jnp.bfloat16)
    gathered = lax.all_gather(outgoing, "ctx", axis=0, tiled=True)
    produced = lax.psum_scatter(
        expert_part(gathered, gate_cols, up_cols, down_rows).astype(jnp.bfloat16),
        "ctx",
        scatter_dimension=0,
        tiled=True,
    ).astype(jnp.float32)
    spread_back = jnp.einsum("ecn,cd->nd", weighted, produced, precision=lax.Precision.HIGHEST)
    mixture = lax.psum_scatter(
        spread_back.astype(jnp.bfloat16), "exp", scatter_dimension=0, tiled=True
    ).astype(jnp.float32)
    hidden = lax.dynamic_slice_in_dim(hidden_all, first_mine, group_rows, 0)
    return (hidden + mixture).astype(jnp.bfloat16)


def solution(mesh):
    in_specs = (
        P("ctx", "exp"),
        P("ctx", "exp"),
        P("ctx", "exp"),
        P("ctx", "exp"),
        P("exp"),
        P("exp"),
        P("exp", None),
        P(("ctx", "exp"), None),
        P(),
        P("ctx", None),
        P("ctx", None),
        P("exp", "ctx", None),
        P("exp", "ctx", None),
        P("exp", "ctx", None),
    )
    out_specs = P(("ctx", "exp"), None)
    return jax.shard_map(body, mesh=mesh, in_specs=in_specs, out_specs=out_specs, check_vma=False)
```

profile of v0, /device:TPU:0, one launch (start us, length us, event | category | flops | bytes accessed | tf_op | source)
XLA Modules:
  0.0 522.2 jit_solution(2067149946234657723)
XLA Ops:
  7.9 2.1 copy.36
  10.7 2.2 convolution_convert_fusion.3
  15.6 69.3 %all-reduce = bf16[256]{0:T(256)(128)(2,1)S(1)} all-reduce(bf16[256]{0:T(256)(128)(2,1)S(1)} %dynamic-update-slice.1), channel_id=2, replica_groups=mesh['ctx'=32,'exp'=4] {'ctx'}, use_global_device_ids=true, to_apply=%add | all-reduce | flops 256 | bytes 1024
  85.6 2.3 add_divide_fusion
  87.9 2.6 copy.34
  92.0 86.4 %while.14 = (s32[]{:T(128)}, f32[8,128,128]{2,1,0:T(8,128)}, s32[]{:T(128)}, bf16[32,8]{1,0:T(8,128)(2,1)}, bf16[32,8,128,128]{3,2,1,0:T(8,128)(2,1)}, /*index=5*/s32[]{:T(128)}, s32[]{:T(128)}) while((s32[]{:T(128)}, f32[8,128,128]{2,1,0:T(8,128)}, s32[]{:T(128)}, bf16[32,8]{1,0:T(8,128)(2,1)}, ...), condition=%wide.region_1.2_spmd.clone, body=%wide.region_0.1_spmd.clone.sunk | while | flops 655372 | bytes 1310905 | solution.py:29
  95.3 2.0 fusion.70
  98.0 2.0 fusion.70
  173.7 2.0 fusion.70
  178.5 3.6 convolution_bitcast_fusion
  182.0 3.7 multiply_reduce_fusion.1
  187.5 6.7 %fusion.57 = f32[256,6144]{1,0:T(8,128)S(1)} fusion(bf16[256,1024]{0,1:T(8,128)(2,1)S(1)} %bitcast.89, bf16[1024,6144]{1,0:T(8,128)(2,1)} %param.22), kind=kOutput, calls=%fused_computation.78 | convolution fusion | flops 3221225472 | bytes 19398656 | tf_op jit(solution)/shard_map/dot_general | solution.py:143
  194.5 2.1 convert_element_type.110
  197.5 71.4 %all-reduce.3.cloned.1.call-done = bf16[256,6144]{1,0:T(8,128)(2,1)} async-done(((bf16[256,6144]{1,0:T(8,128)(2,1)}), bf16[256,6144]{1,0:T(8,128)(2,1)}) %all-reduce.3.cloned.1.call-update) | async-done | bytes 3145744 | tf_op jit(solution)/shard_map/psum | solution.py:144
  268.8 2.6 multiply_reduce_fusion
  271.4 3.7 convolution_convert_fusion.2
  275.4 62.7 %all-gather.5.cloned.1.call-done = bf16[1024,6144]{1,0:T(8,128)(2,1)} async-done(((bf16[32,6144]{1,0:T(8,128)(2,1)}), bf16[1024,6144]{1,0:T(8,128)(2,1)}) %all-gather.5.cloned.1.call-update) | async-done | bytes 12582928 | tf_op jit(solution)/shard_map/all_gather | solution.py:151
  338.0 10.5 %fusion.4 = f32[1024,288]{0,1:T(8,128)} fusion(bf16[1024,6144]{1,0:T(8,128)(2,1)} %all-gather.5.cloned.1.call-done, bf16[1,288,6144]{2,1,0:T(8,128)(2,1)} %param.27), kind=kOutput, calls=%fused_computation.11 | convolution fusion | flops 3623878656 | bytes 17301504 | tf_op jit(solution)/shard_map/dot_general | solution.py:93
  348.5 17.6 %convolution_convert_fusion = bf16[1024,6144]{1,0:T(8,128)(2,1)} fusion(bf16[1,288,6144]{2,1,0:T(8,128)(2,1)S(1)} %copy-done, bf16[1024,6144]{1,0:T(8,128)(2,1)} %all-gather.5.cloned.1.call-done, bf16[1,288,6144]{2,1,0:T(8,128)(2,1)} %param.28, f32[1024,288]{0,1:T(8,128)} %fusion.4), kind=kOutput, calls=%fused_computation.3 | convolution fusion | flops 7255818240 | bytes 33423360 | tf_op jit(solution)/shard_map/dot_general | solution.py:100
  366.8 103.4 %reduce-scatter.3.cloned.1.call-done = bf16[32,6144]{1,0:T(8,128)(2,1)} async-done(((bf16[1024,6144]{1,0:T(8,128)(2,1)}), bf16[32,6144]{1,0:T(8,128)(2,1)}) %reduce-scatter.3.cloned.1.call-update) | async-done | bytes 393232 | tf_op jit(solution)/shard_map/reduce_scatter | solution.py:152
  470.2 5.1 convolution_convert_fusion.1
  475.4 5.4 %convert_element_type.111 = f32[256,6144]{1,0:T(8,128)} convert(bf16[256,6144]{1,0:T(8,128)(2,1)} %all-reduce.3.cloned.1.call-done) | non-fusion elementwise | flops 1572864 | bytes 9437184 | tf_op jit(solution)/shard_map/convert_element_type | solution.py:144
  480.8 32.2 %reduce-scatter.5.cloned.1.call-done = bf16[64,6144]{1,0:T(8,128)(2,1)} async-done(((bf16[256,6144]{1,0:T(8,128)(2,1)}), bf16[64,6144]{1,0:T(8,128)(2,1)}) %reduce-scatter.5.cloned.1.call-update) | async-done | bytes 786448 | tf_op jit(solution)/shard_map/reduce_scatter | solution.py:159
  513.0 2.7 add_convert_fusion
  (109 shorter events, 90.5 us)
Async XLA Ops:
  6.5 342.0 %copy-start = (bf16[1,288,6144]{2,1,0:T(8,128)(2,1)S(1)}, bf16[1,288,6144]{2,1,0:T(8,128)(2,1)}, u32[]{:S(2)}) copy-start(bf16[1,288,6144]{2,1,0:T(8,128)(2,1)} %param.29) | copy-start | bytes 10616836
  6.5 85.5 %all-gather.7.cloned.1.call-start = ((), (), s32[]{:S(2)}) async-start(), calls=%async_computation.6 | async-start | bytes 8650752 | tf_op jit(solution)/shard_map/all_gather | solution.py:12
  12.9 255.9 %all-reduce.3.cloned.1.call-start = ((), (), s32[]{:S(2)}) async-start(), calls=%async_computation.2 | async-start | bytes 6291456 | tf_op jit(solution)/shard_map/psum | solution.py:144
  92.0 90.0 %copy-start.6 = (f32[8]{0:T(128)S(1)}, f32[8]{0:T(128)}, u32[]{:S(2)}) copy-start(f32[8]{0:T(128)} %get-tuple-element.131) | copy-start | bytes 100
  178.5 7.3 %copy-start.3 = (f32[1024]{0:T(1024)S(1)}, f32[1024]{0:T(1024)}, u32[]{:S(2)}) copy-start(f32[1024]{0:T(1024)} %param.21) | copy-start | bytes 12292
  187.5 6.7 %copy-start.2 = (bf16[64,6144]{1,0:T(8,128)(2,1)S(1)}, bf16[64,6144]{1,0:T(8,128)(2,1)}, u32[]{:S(2)}) copy-start(bf16[64,6144]{1,0:T(8,128)(2,1)} %param.23) | copy-start | bytes 2359300
  194.5 2.2 copy-start.5
  196.6 141.4 %all-gather.5.cloned.1.call-start = ((), (), s32[]{:S(2)}) async-start(), calls=%async_computation.3 | async-start | bytes 12976128 | tf_op jit(solution)/shard_map/all_gather | solution.py:151
  275.1 195.1 %reduce-scatter.3.cloned.1.call-start = ((), (), s32[]{:S(2)}) async-start(), calls=%async_computation.4 | async-start | bytes 12976128 | tf_op jit(solution)/shard_map/reduce_scatter | solution.py:152
  366.2 0.7 copy-start.4
  366.2 146.9 %reduce-scatter.5.cloned.1.call-start = ((), (), s32[]{:S(2)}) async-start(), calls=%async_computation.5 | async-start | bytes 3932160 | tf_op jit(solution)/shard_map/reduce_scatter | solution.py:159
  475.4 40.3 %copy-start.1 = (bf16[1,288,6144]{2,1,0:T(8,128)(2,1)S(1)}, bf16[1,288,6144]{2,1,0:T(8,128)(2,1)}, u32[]{:S(2)}) copy-start(bf16[1,288,6144]{2,1,0:T(8,128)(2,1)} %param.29) | copy-start | bytes 10616836
Sparse Core Ops, SparseCore 0:
  13.0 55.7 all-gather.6
  196.7 72.0 all-reduce.2
  275.2 62.7 all-gather.4
  366.3 103.8 reduce-scatter.2
  475.5 37.5 reduce-scatter.4
where the time goes:
time: 525 us; the launch traced here: 522 us
  waiting for transfers between devices  270 us (51%)
  other arithmetic  108 us (21%)
  blocking collectives  69.3 us (13%)
  matrix products  53 us (10%)
  between operations  13.8 us (3%)
  local copies, waits for them, and re-layouts  8.36 us (2%)
    reduce_scatter x1, waiting for transfers between devices, body(): lax.psum_scatter(expert_part(gathered, gate_cols, up_cols, down_rows).ast...  103 us
    psum x1, waiting for transfers between devices, body(): lax.psum(projected.astype(jnp.bfloat16), 'exp').astype(jnp.float32)  71.4 us
    unnamed x1, blocking collectives  69.3 us
    select_n x32, other arithmetic, turn(): return jax.tree.map(lambda a, b: jnp.where(reached, a, b), new, before)  65.1 us
    all_gather x1, waiting for transfers between devices, body(): gathered = lax.all_gather(outgoing, 'ctx', axis=0, tiled=True)  62.7 us
    reduce_scatter x1, waiting for transfers between devices, body(): lax.psum_scatter(spread_back.astype(jnp.bfloat16), 'exp', scatter_dimensi...  32.2 us
    convert_element_type x32, other arithmetic, turn(): part[k].astype(own.dtype)  21.3 us
    dot_general x1, matrix products, expert_part(): return jnp.dot(activated, down_rows, preferred_element_type=jnp.float32)  17.6 us
  transfers between devices with their start and end apart: 5, of which 4 were waited for; matrix products, arithmetic and copies ran while one was open for 3% of the time, Pallas kernels for 0%

commit v1 on v0

v1 whole, which is shorter than its diff:
```python
import jax
import jax.numpy as jnp
from jax import lax
from jax.sharding import PartitionSpec as P

EPSILON = 1e-06


def earlier_states(update, decay_rates, row_count):
    size, index = (lax.axis_size("ctx"), lax.axis_index("ctx"))
    everything = lax.all_gather(update.astype(jnp.bfloat16), "ctx").astype(jnp.float32)
    distance = (index - 1 - jnp.arange(size)).astype(jnp.float32)
    factors = jnp.where(
        distance[:, None] >= 0.0,
        jnp.exp(-decay_rates[None, :] * row_count * jnp.maximum(distance, 0.0)[:, None]),
        0.0,
    )
    return jnp.sum(everything * factors[:, :, None, None], axis=0)


def span_local(queries, key_rows, value_rows, decay_exp):
    row_count = queries.shape[0]
    head_count = decay_exp.shape[0]
    head_width = queries.shape[1] // head_count
    query_heads = queries.reshape(row_count, head_count, head_width)
    key_heads = key_rows.reshape(row_count, head_count, head_width)
    value_heads = value_rows.reshape(row_count, head_count, head_width)
    decay_rates = jnp.exp2(-decay_exp.astype(jnp.float32))
    positions = jnp.arange(row_count, dtype=jnp.float32)
    offsets = positions[:, None] - positions[None, :]
    damping = jnp.where(
        offsets[None] >= 0.0,
        jnp.exp(-decay_rates[:, None, None] * jnp.maximum(offsets, 0.0)[None]),
        0.0,
    )
    scores = jnp.einsum("thd,shd->hts", query_heads, key_heads, preferred_element_type=jnp.float32)
    mixing = (scores * damping).astype(jnp.bfloat16)
    inner_part = jnp.einsum("hts,shd->thd", mixing, value_heads, preferred_element_type=jnp.float32)
    tail_decay = jnp.exp(-decay_rates[None, :] * (row_count - 1.0 - positions)[:, None])
    keyed_rows = (key_heads.astype(jnp.float32) * tail_decay[:, :, None]).astype(jnp.bfloat16)
    update = jnp.einsum("shd,she->hde", keyed_rows, value_heads, preferred_element_type=jnp.float32)
    lead_decay = jnp.exp(-decay_rates[None, :] * (positions + 1.0)[:, None])
    leading = query_heads.astype(jnp.float32) * lead_decay[:, :, None]
    return (inner_part, leading, update, decay_rates)


def settle(inner_part, leading, prior_state, gate_rows, attn_gain):
    outer_part = jnp.einsum("thd,hde->the", leading, prior_state, precision=lax.Precision.HIGHEST)
    mixed_heads = inner_part + outer_part
    row_count, head_count, head_width = mixed_heads.shape
    mean_square = jnp.mean(mixed_heads * mixed_heads, axis=2, keepdims=True)
    normed_heads = mixed_heads * lax.rsqrt(mean_square + EPSILON)
    gain_heads = attn_gain.reshape(head_count, head_width)
    gate_heads = gate_rows.reshape(row_count, head_count, head_width).astype(jnp.float32)
    settled = (normed_heads * gain_heads * jax.nn.sigmoid(gate_heads)).astype(jnp.bfloat16)
    return settled.reshape(row_count, head_count * head_width)


def token_norm(hidden, norm_gain):
    mean_square = jnp.mean(hidden * hidden, axis=1, keepdims=True)
    return (hidden * lax.rsqrt(mean_square + EPSILON) * norm_gain).astype(jnp.bfloat16)


def slot_table(chosen_ids, expert_count, capacity):
    owners = jnp.arange(expert_count, dtype=jnp.int32)
    chosen = jnp.where(owners[:, None] % 2 == 0, chosen_ids[None, :, 0], chosen_ids[None, :, 1])
    picked = chosen == owners[:, None]
    row_count = chosen_ids.shape[0]
    upto = jnp.arange(row_count)[:, None] <= jnp.arange(row_count)[None, :]
    slot_rank = jnp.dot(picked.astype(jnp.float32), upto.astype(jnp.float32)) - 1.0
    slot_ids = jnp.arange(capacity, dtype=jnp.float32)
    return picked[:, None, :] & (slot_rank[:, None, :] == slot_ids[None, :, None])


def expert_part(slot_rows, gate_cols, up_cols, down_rows):
    contract_dims = (((1,), (1,)), ((), ()))
    first_half = lax.dot_general(
        slot_rows, gate_cols, contract_dims, preferred_element_type=jnp.float32
    )
    second_half = lax.dot_general(
        slot_rows, up_cols, contract_dims, preferred_element_type=jnp.float32
    )
    activated = (jax.nn.silu(first_half) * second_half).astype(jnp.bfloat16)
    return jnp.dot(activated, down_rows, preferred_element_type=jnp.float32)


def body(
    queries,
    key_rows,
    value_rows,
    gate_rows,
    decay_exp,
    attn_gain,
    out_proj,
    residual,
    norm_gain,
    routes,
    route_weights,
    w_gate,
    w_up,
    w_down,
):
    inner_part, leading, update, decay_rates = span_local(
        queries, key_rows, value_rows, decay_exp
    )
    span_rows = queries.shape[0]
    prior_state = earlier_states(update, decay_rates, span_rows)
    settled = settle(inner_part, leading, prior_state, gate_rows, attn_gain)
    group_count = lax.axis_size("exp")
    group_rows = span_rows // group_count
    first_mine = lax.axis_index("exp") * group_rows
    capacity = group_rows // 8
    projected = jnp.dot(settled, out_proj, preferred_element_type=jnp.float32)
    summed = lax.psum_scatter(
        projected.astype(jnp.bfloat16), "exp", scatter_dimension=0, tiled=True
    ).astype(jnp.float32)
    hidden = summed + residual.astype(jnp.float32)
    normed = token_norm(hidden, norm_gain)
    my_routes = lax.dynamic_slice_in_dim(routes, first_mine, group_rows, 0)
    my_weights = lax.dynamic_slice_in_dim(route_weights, first_mine, group_rows, 0)
    table = slot_table(my_routes, group_count, capacity)
    outgoing = jnp.einsum(
        "ecn,nd->ecd", table.astype(jnp.bfloat16), normed, preferred_element_type=jnp.float32
    ).astype(jnp.bfloat16)
    mine = lax.all_to_all(outgoing, "exp", 0, 0, tiled=True)
    mine = mine.reshape(group_count * capacity, -1)
    gathered = lax.all_gather(mine, "ctx", axis=0, tiled=True)
    produced = lax.psum_scatter(
        expert_part(gathered, w_gate[0], w_up[0], w_down[0]).astype(jnp.bfloat16),
        "ctx",
        scatter_dimension=0,
        tiled=True,
    )
    produced = produced.reshape(group_count, capacity, -1)
    returned = lax.all_to_all(produced, "exp", 0, 0, tiled=True)
    for column in range(2):
        fetched = jnp.einsum(
            "ecn,ecd->nd",
            table[column::2].astype(jnp.bfloat16),
            returned[column::2],
            preferred_element_type=jnp.float32,
        )
        hidden = hidden + my_weights[:, column][:, None] * fetched
    return hidden.astype(jnp.bfloat16)


def solution(mesh):
    in_specs = (
        P("ctx", "exp"),
        P("ctx", "exp"),
        P("ctx", "exp"),
        P("ctx", "exp"),
        P("exp"),
        P("exp"),
        P("exp", None),
        P(("ctx", "exp"), None),
        P(),
        P("ctx", None),
        P("ctx", None),
        P("exp", "ctx", None),
        P("exp", "ctx", None),
        P("exp", "ctx", None),
    )
    out_specs = P(("ctx", "exp"), None)
    return jax.shard_map(body, mesh=mesh, in_specs=in_specs, out_specs=out_specs, check_vma=False)
```

time: 525 us -> 363 us (0.69)
  other arithmetic: 108 us -> 15.3 us
  blocking collectives: 69.3 us -> 11.5 us
  waiting for transfers between devices: 270 us -> 258 us
    psum x1 -> x0, waiting for transfers between devices: 71.4 us -> none  [body(): lax.psum(projected.astype(jnp.bfloat16), 'exp').astype(jnp.float32)]
    unnamed x1 -> x0, blocking collectives: 69.3 us -> none
    select_n x33 -> x1, other arithmetic: 65.1 us -> 0.74 us  [earlier_states(): jnp.where(distance[:, None] >= 0.0, jnp.exp(-decay_rates[None, :] * row_c...]
    all_gather x2, waiting for transfers between devices: 62.7 us -> 111 us  [the longest x1 62.3 us: body(): gathered = lax.all_gather(mine, 'ctx', axis=0, tiled=True)]
    convert_element_type x37 -> x0, other arithmetic: 32.9 us -> none  [the longest x32 21.3 us: turn(): part[k].astype(own.dtype)]
    all_to_all x0 -> x1, blocking collectives: none -> 11.5 us  [body(): mine = lax.all_to_all(outgoing, 'exp', 0, 0, tiled=True)]
    all_to_all x0 -> x1, waiting for transfers between devices: none -> 6.86 us  [body(): returned = lax.all_to_all(produced, 'exp', 0, 0, tiled=True)]
    dot_general x3 -> x5, matrix products: 15.4 us -> 15.7 us  [the longest x1 9.51 us: body(): projected = jnp.dot(settled, out_proj, preferred_element_type=jnp.float32)]
  transfers between devices with their start and end apart: 5 -> 5, of which waited for: 4 -> 5; matrix products, arithmetic and copies ran while one was open for 3% -> 2% of each run, Pallas kernels for 0% -> 0%
where the time goes in v1:
time: 363 us; the launch traced here: 362 us
  waiting for transfers between devices  258 us (71%)
  matrix products  52.1 us (14%)
  other arithmetic  15.3 us (4%)
  between operations  13.2 us (4%)
  blocking collectives  11.5 us (3%)
  local copies, waits for them, and re-layouts  7.34 us (2%)
  starting transfers between devices  4.58 us (1%)
    reduce_scatter x1, waiting for transfers between devices, body(): lax.psum_scatter(expert_part(gathered, w_gate[0], w_up[0], w_down[0]).ast...  103 us
    all_gather x1, waiting for transfers between devices, body(): gathered = lax.all_gather(mine, 'ctx', axis=0, tiled=True)  62.3 us
    all_gather x1, waiting for transfers between devices, earlier_states(): lax.all_gather(update.astype(jnp.bfloat16), 'ctx').astype(jnp.float32)  48.4 us
    reduce_scatter x1, waiting for transfers between devices, body(): lax.psum_scatter(projected.astype(jnp.bfloat16), 'exp', scatter_dimension...  37 us
    dot_general x1, matrix products, expert_part(): return jnp.dot(activated, down_rows, preferred_element_type=jnp.float32)  17.6 us
    all_to_all x1, blocking collectives, body(): mine = lax.all_to_all(outgoing, 'exp', 0, 0, tiled=True)  11.5 us
    dot_general x1, matrix products, expert_part(): lax.dot_general(slot_rows, gate_cols, contract_dims, preferred_element_ty...  10.5 us
    dot_general x1, matrix products, body(): projected = jnp.dot(settled, out_proj, preferred_element_type=jnp.float32)  9.51 us
  transfers between devices with their start and end apart: 5, of which 5 were waited for; matrix products, arithmetic and copies ran while one was open for 2% of the time, Pallas kernels for 0%

profile of v1, /device:TPU:0, one launch (start us, length us, event | category | flops | bytes accessed | tf_op | source)
XLA Modules:
  0.0 362.1 jit_solution(7711785279852202598)
XLA Ops:
  6.5 1.4 broadcast_multiply_fusion
  7.9 2.0 copy.27
  10.7 2.2 convolution_convert_fusion.3
  13.0 2.3 add_divide_fusion
  15.2 2.6 copy.25
  18.6 0.8 fusion.45
  20.1 48.4 %all-gather.6.cloned.1.call-done = bf16[256,128,128]{2,1,0:T(8,128)(2,1)} async-done(((bf16[8,128,128]{2,1,0:T(8,128)(2,1)}), bf16[256,128,128]{2,1,0:T(8,128)(2,1)}) %all-gather.6.cloned.1.call-update) | async-done | bytes 8388624 | tf_op jit(solution)/shard_map/all_gather | solution.py:11
  68.5 5.2 %fusion = f32[8,128,128]{2,1,0:T(8,128)S(1)} fusion(bf16[32,8,128,128]{3,2,1,0:T(8,128)(2,1)} %bitcast.93, f32[32,8]{1,0:T(8,128)S(1)} %exponential_select_fusion), kind=kLoop, calls=%fused_computation.1 | loop fusion | flops 12451840 | bytes 8913920 | tf_op jit(solution)/shard_map/reduce_sum | solution.py:18
  73.7 2.4 convolution_bitcast_fusion.2
  76.1 3.7 %multiply_reduce_fusion.1 = (f32[256,8]{0,1:T(8,128)S(1)}, f32[256,8,128]{0,2,1:T(8,128)}) fusion(f32[256,8,128]{0,2,1:T(8,128)} %convolution_bitcast_fusion.2, bf16[256,8,128]{0,2,1:T(8,128)(2,1)} %bitcast.98, f32[256,256]{1,0:T(8,128)} %fusion.45, f32[8]{0:T(128)S(1)} %copy-done.7, pred[256,256]{1,0:T(8,128)(4,1)} %fusion.46, ...), kind=kOutput, calls=%fused_computation.31 | convolution fusion | flops 271316992 | bytes 4005920 | tf_op jit(solution)/shard_map/hts,shd->thd/dot_general | solution.py:38
  79.8 1.8 multiply_convert_fusion.2
  81.6 9.5 %convolution_convert_fusion.1 = bf16[256,6144]{1,0:T(8,128)(2,1)} fusion(bf16[256,1024]{0,1:T(8,128)(2,1)S(1)} %bitcast.95, bf16[1024,6144]{1,0:T(8,128)(2,1)} %param.20), kind=kOutput, calls=%fused_computation.3 | convolution fusion | flops 3222798336 | bytes 16252928 | tf_op jit(solution)/shard_map/dot_general | solution.py:113
  92.1 37.0 %reduce-scatter.3.cloned.1.call-done = bf16[64,6144]{1,0:T(8,128)(2,1)} async-done(((bf16[256,6144]{1,0:T(8,128)(2,1)}), bf16[64,6144]{1,0:T(8,128)(2,1)}) %reduce-scatter.3.cloned.1.call-update) | async-done | bytes 786448 | tf_op jit(solution)/shard_map/reduce_scatter | solution.py:114
  129.1 1.7 multiply_reduce_fusion
  130.9 1.8 convolution_convert_fusion.2
  132.7 11.5 %all_to_all.10 = bf16[4,8,6144]{2,1,0:T(8,128)(2,1)} all-to-all(bf16[4,8,6144]{2,1,0:T(8,128)(2,1)S(1)} %convolution_convert_fusion.2), channel_id=1, replica_groups=mesh['ctx'=32,'exp'=4] {'exp'}, dimensions={0} | all-to-all | bytes 786432 | tf_op jit(solution)/shard_map/all_to_all | solution.py:125
  144.4 62.3 %all-gather.4.cloned.1.call-done = bf16[1024,6144]{1,0:T(8,128)(2,1)} async-done(((bf16[32,6144]{1,0:T(8,128)(2,1)}), bf16[1024,6144]{1,0:T(8,128)(2,1)}) %all-gather.4.cloned.1.call-update) | async-done | bytes 12582928 | tf_op jit(solution)/shard_map/all_gather | solution.py:127
  206.7 10.5 %fusion.9 = f32[1024,288]{0,1:T(8,128)} fusion(bf16[1024,6144]{1,0:T(8,128)(2,1)} %all-gather.4.cloned.1.call-done, bf16[1,288,6144]{2,1,0:T(8,128)(2,1)} %param.25), kind=kOutput, calls=%fused_computation.15 | convolution fusion | flops 3623878656 | bytes 17301504 | tf_op jit(solution)/shard_map/dot_general | solution.py:77
  217.2 17.6 %convolution_convert_fusion = bf16[1024,6144]{1,0:T(8,128)(2,1)} fusion(bf16[1,288,6144]{2,1,0:T(8,128)(2,1)S(1)} %copy-done, bf16[1024,6144]{1,0:T(8,128)(2,1)} %all-gather.4.cloned.1.call-done, bf16[1,288,6144]{2,1,0:T(8,128)(2,1)} %param.26, f32[1024,288]{0,1:T(8,128)} %fusion.9), kind=kOutput, calls=%fused_computation.2 | convolution fusion | flops 7255818240 | bytes 33423360 | tf_op jit(solution)/shard_map/dot_general | solution.py:84
  235.6 103.3 %reduce-scatter.5.cloned.1.call-done = bf16[32,6144]{1,0:T(8,128)(2,1)} async-done(((bf16[1024,6144]{1,0:T(8,128)(2,1)}), bf16[32,6144]{1,0:T(8,128)(2,1)}) %reduce-scatter.5.cloned.1.call-update) | async-done | bytes 393232 | tf_op jit(solution)/shard_map/reduce_scatter | solution.py:128
  338.9 4.3 %all-to-all-start.1 = ((bf16[4,8,6144]{2,1,0:T(8,128)(2,1)}), bf16[4,8,6144]{2,1,0:T(8,128)(2,1)S(1)}, u32[]{:S(2)}, u32[]{:S(2)}) async-start(bf16[4,8,6144]{2,1,0:T(8,128)(2,1)} %bitcast.99), calls=%async_computation.3 | async-start | bytes 786432 | tf_op jit(solution)/shard_map/all_to_all | solution.py:135
  343.7 6.9 %all-to-all-done.1 = bf16[4,8,6144]{2,1,0:T(8,128)(2,1)S(1)} async-done(((bf16[4,8,6144]{2,1,0:T(8,128)(2,1)}), bf16[4,8,6144]{2,1,0:T(8,128)(2,1)S(1)}, u32[]{:S(2)}, u32[]{:S(2)}) %all-to-all-start.1) | async-done | bytes 393248 | tf_op jit(solution)/shard_map/all_to_all | solution.py:135
  351.3 1.5 fusion.4
  352.8 2.8 fusion.5
  (44 shorter events, 5.4 us)
Async XLA Ops:
  6.5 210.7 %copy-start = (bf16[1,288,6144]{2,1,0:T(8,128)(2,1)S(1)}, bf16[1,288,6144]{2,1,0:T(8,128)(2,1)}, u32[]{:S(2)}) copy-start(bf16[1,288,6144]{2,1,0:T(8,128)(2,1)} %param.27) | copy-start | bytes 10616836
  6.5 62.0 %all-gather.6.cloned.1.call-start = ((), (), s32[]{:S(2)}) async-start(), calls=%async_computation.7 | async-start | bytes 8650752 | tf_op jit(solution)/shard_map/all_gather | solution.py:11
  7.9 7.3 %copy-start.6 = (f32[8]{0:T(128)}, f32[8]{0:T(128)S(1)}, u32[]{:S(2)}) copy-start(f32[8]{0:T(128)S(1)} %get-tuple-element.6) | copy-start | bytes 100
  12.9 116.2 %reduce-scatter.3.cloned.1.call-start = ((), (), s32[]{:S(2)}) async-start(), calls=%async_computation.4 | async-start | bytes 3932160 | tf_op jit(solution)/shard_map/reduce_scatter | solution.py:114
  68.5 5.2 %copy-start.3 = (bf16[256,1024]{1,0:T(8,128)(2,1)S(1)}, bf16[256,1024]{1,0:T(8,128)(2,1)}, u32[]{:S(2)}) copy-start(bf16[256,1024]{1,0:T(8,128)(2,1)} %param.14) | copy-start | bytes 1572868
  68.5 5.2 %copy-start.4 = (f32[256,8]{0,1:T(8,128)S(1)}, f32[256,8]{0,1:T(8,128)}, u32[]{:S(2)}) copy-start(f32[256,8]{0,1:T(8,128)} %get-tuple-element.11) | copy-start | bytes 24580
  73.7 2.4 copy-start.7
  76.1 3.7 %copy-start.5 = (f32[1024]{0:T(1024)S(1)}, f32[1024]{0:T(1024)}, u32[]{:S(2)}) copy-start(f32[1024]{0:T(1024)} %param.19) | copy-start | bytes 12292
  91.1 0.7 copy-start.8
  91.1 115.6 %all-gather.4.cloned.1.call-start = ((), (), s32[]{:S(2)}) async-start(), calls=%async_computation.5 | async-start | bytes 12976128 | tf_op jit(solution)/shard_map/all_gather | solution.py:127
  144.2 194.7 %reduce-scatter.5.cloned.1.call-start = ((), (), s32[]{:S(2)}) async-start(), calls=%async_computation.6 | async-start | bytes 12976128 | tf_op jit(solution)/shard_map/reduce_scatter | solution.py:128
  234.8 0.7 copy-start.9
  338.9 11.7 %all-to-all-start.1 = ((bf16[4,8,6144]{2,1,0:T(8,128)(2,1)}), bf16[4,8,6144]{2,1,0:T(8,128)(2,1)S(1)}, u32[]{:S(2)}, u32[]{:S(2)}) async-start(bf16[4,8,6144]{2,1,0:T(8,128)(2,1)} %bitcast.99), calls=%async_computation.3 | async-start | bytes 786432 | tf_op jit(solution)/shard_map/all_to_all | solution.py:135
  350.5 0.7 copy-start.2
  351.3 4.3 %copy-start.1 = (bf16[1,288,6144]{2,1,0:T(8,128)(2,1)S(1)}, bf16[1,288,6144]{2,1,0:T(8,128)(2,1)}, u32[]{:S(2)}) copy-start(bf16[1,288,6144]{2,1,0:T(8,128)(2,1)} %param.27) | copy-start | bytes 10616836
Sparse Core Ops, SparseCore 0:
  13.0 55.4 all-gather.5
  91.2 37.8 reduce-scatter.2
  144.3 62.3 all-gather.3
  235.0 103.8 reduce-scatter.4

commit v2 on v1

--- a/solution.py
+++ b/solution.py
@@ -1,6 +1,10 @@
+import functools
+
 import jax
 import jax.numpy as jnp
 from jax import lax
+from jax.experimental import pallas as pl
+from jax.experimental.pallas import tpu as pltpu
 from jax.sharding import PartitionSpec as P
 
 EPSILON = 1e-06
@@ -72,16 +76,321 @@
     return picked[:, None, :] & (slot_rank[:, None, :] == slot_ids[None, :, None])
 
 
-def expert_part(slot_rows, gate_cols, up_cols, down_rows):
-    contract_dims = (((1,), (1,)), ((), ()))
-    first_half = lax.dot_general(
-        slot_rows, gate_cols, contract_dims, preferred_element_type=jnp.float32
-    )
-    second_half = lax.dot_general(
-        slot_rows, up_cols, contract_dims, preferred_element_type=jnp.float32
-    )
-    activated = (jax.nn.silu(first_half) * second_half).astype(jnp.bfloat16)
-    return jnp.dot(activated, down_rows, preferred_element_type=jnp.float32)
+MESH = pl.DeviceIdType.MESH
+BF16 = jnp.bfloat16
+F32 = jnp.float32
+RING = 4
+CHUNKS = 3
+WIDTH = 512
+SLOTS = 32
+
+
+def place(index):
+    return index // 8, (index // 2) % 4, index % 2
+
+
+class Copies:
+    def __init__(self, send_sems, recv_sems, owner):
+        self.send_sems, self.recv_sems, self.owner = send_sems, recv_sems, owner
+        self.count, self.started = 0, []
+
+    def start(self, source, target, ctx):
+        copy = pltpu.make_async_remote_copy(
+            src_ref=source,
+            dst_ref=target,
+            send_sem=self.send_sems.at[self.count],
+            recv_sem=self.recv_sems.at[self.count],
+            device_id=(ctx, self.owner),
+            device_id_type=MESH,
+        )
+        copy.start()
+        self.count += 1
+        self.started.append(copy)
+        return copy
+
+    def finish(self):
+        for copy in self.started:
+            copy.wait_send()
+
+
+def experts_kernel(
+    slots, w_gate, w_up, w_down, out,
+    rows, w_in, w_out, pre, act, part, in1, comb1, mid, in2, comb2,
+    send_sems, recv_sems, local_sems,
+):
+    index, owner = lax.axis_index("ctx"), lax.axis_index("exp")
+    z, x, core = place(index)
+
+    def device(zz, xx):
+        return zz * 8 + xx * 2 + core
+
+    x_right, x_left = lax.rem(x + 1, RING), lax.rem(x + 3, RING)
+    z_right, z_left = lax.rem(z + 1, RING), lax.rem(z + 3, RING)
+    partner = index + 1 - 2 * core
+    near = {
+        "x": (x, x_left, x_right, device(z, x_left), device(z, x_right), lax.rem(x + 2, RING)),
+        "z": (z, z_left, z_right, device(z_left, x), device(z_right, x), lax.rem(z + 2, RING)),
+    }
+    barrier = pltpu.get_barrier_semaphore()
+    for other in (partner, near["x"][3], near["x"][4], near["z"][3], near["z"][4]):
+        pl.semaphore_signal(barrier, inc=1, device_id=(other, owner), device_id_type=MESH)
+    pl.semaphore_wait(barrier, 5)
+    copies = Copies(send_sems, recv_sems, owner)
+    units = w_gate.shape[0]
+
+    first, second = ("x", "z"), ("z", "x")
+    pairs = [(c, h) for c in range(CHUNKS) for h in range(2)]
+    gather1, relay1, gather2, relay2, own = {}, {}, {}, {}, {}
+
+    def line(c, h, stage, sub, at):
+        axis = (first if stage == 1 else second)[h]
+        if stage == 1:
+            return rows.at[c, h, sub, at, x] if axis == "z" else rows.at[c, h, sub, z, at]
+        return rows.at[c, h, sub, at] if axis == "z" else rows.at[c, h, sub, :, at]
+
+    both = slice(None)
+    for n, (c, h) in enumerate(pairs):
+        me, left, right, to_left, to_right, far = near[first[h]]
+        mine = line(c, h, 1, both, me)
+        gather1[c, h] = (
+            copies.start(slots.at[c, h], mine, to_right),
+            copies.start(slots.at[c, h], mine, to_left),
+        )
+        own[c, h] = pltpu.make_async_copy(slots.at[c, h], mine, local_sems.at[n])
+        own[c, h].start()
+
+    weight_copies, weight_shares = [], []
+    for n, (source, target, base) in enumerate(
+        ((w_gate, w_in, 0), (w_up, w_in, 2 * units), (w_down, w_out, 0))
+    ):
+        copy = pltpu.make_async_copy(
+            source, target.at[pl.ds(base, units)], local_sems.at[len(pairs) + n]
+        )
+        copy.start()
+        weight_copies.append(copy)
+        weight_shares.append(copies.start(source, target.at[pl.ds(base + units, units)], partner))
+
+    def pass_on1(c, h):
+        me, left, right, to_left, to_right, far = near[first[h]]
+        from_left, from_right = gather1[c, h]
+        from_left.wait_recv()
+        source = line(c, h, 1, 0, left)
+        one = copies.start(source, source, to_right)
+        from_right.wait_recv()
+        source = line(c, h, 1, 1, right)
+        relay1[c, h] = (one, copies.start(source, source, to_left))
+
+    def start2(c, h):
+        for copy in relay1[c, h]:
+            copy.wait_recv()
+        own[c, h].wait()
+        me, left, right, to_left, to_right, far = near[second[h]]
+        mine = line(c, h, 2, both, me)
+        gather2[c, h] = (copies.start(mine, mine, to_right), copies.start(mine, mine, to_left))
+
+    def pass_on2(c, h):
+        me, left, right, to_left, to_right, far = near[second[h]]
+        from_left, from_right = gather2[c, h]
+        from_left.wait_recv()
+        source = line(c, h, 2, 0, left)
+        one = copies.start(source, source, to_right)
+        from_right.wait_recv()
+        source = line(c, h, 2, 1, right)
+        relay2[c, h] = (one, copies.start(source, source, to_left))
+
+    def multiply_in(c):
+        for h in range(2):
+            for copy in relay2[c, h]:
+                copy.wait_recv()
+        if c == 0:
+            for n in range(2):
+                weight_copies[n].wait()
+                weight_shares[n].wait_recv()
+
+        def tile(t, carry):
+            total = None
+            for h in range(2):
+                for sub in range(2):
+                    block = rows[c, h, sub, pl.ds(2 * t, 2)].reshape(256, WIDTH)
+                    column = ((c * 2 + h) * 2 + sub) * WIDTH
+                    term = lax.dot_general(
+                        w_in[:, column : column + WIDTH],
+                        block,
+                        (((1,), (1,)), ((), ())),
+                        preferred_element_type=F32,
+                    )
+                    total = term if total is None else total + term
+            if c == 0:
+                pre[t] = total
+            else:
+                pre[t] = pre[t] + total
+            return carry
+
+        lax.fori_loop(0, 2, tile, 0)
+
+    for c, h in pairs:
+        pass_on1(c, h)
+    for h in range(2):
+        start2(0, h)
+    for h in range(2):
+        start2(1, h)
+    for h in range(2):
+        start2(2, h)
+    for h in range(2):
+        pass_on2(0, h)
+    for h in range(2):
+        pass_on2(1, h)
+    multiply_in(0)
+    for h in range(2):
+        pass_on2(2, h)
+    multiply_in(1)
+    multiply_in(2)
+
+    def activate(t, carry):
+        gate = pre[t, : 2 * units]
+        up = pre[t, 2 * units :]
+        value = gate / (1.0 + jnp.exp(-gate)) * up
+        act[pl.ds(pl.multiple_of(t * 256, 256), 256), :] = value.T.astype(BF16)
+        return carry
+
+    lax.fori_loop(0, 2, activate, 0)
+    weight_copies[2].wait()
+    weight_shares[2].wait_recv()
+
+    def multiply_out(c):
+        def block(n, carry):
+            column = pl.multiple_of((c * 4 + n) * WIDTH, WIDTH)
+            value = jnp.dot(
+                act[...], w_out[:, pl.ds(column, WIDTH)], preferred_element_type=F32
+            )
+            part[c, n // 2, n % 2] = value.astype(BF16).reshape(RING, RING, SLOTS, WIDTH)
+            return carry
+
+        lax.fori_loop(0, 4, block, 0)
+
+    def piece(c, h, sub, at):
+        return part.at[c, h, sub, at] if second[h] == "z" else part.at[c, h, sub, :, at]
+
+    def scatter(c, h, axis, view, landing):
+        me, left, right, to_left, to_right, far = near[axis]
+        return (
+            copies.start(view(0, far), landing.at[c, h, 0], to_left),
+            copies.start(view(1, far), landing.at[c, h, 1], to_right),
+            copies.start(view(0, right), landing.at[c, h, 2], to_right),
+            copies.start(view(1, left), landing.at[c, h, 3], to_left),
+        )
+
+    def join(c, h, axis, view, landing, staging, sent):
+        me, left, right, to_left, to_right, far = near[axis]
+        joined = []
+        for sub, at, to in ((0, left, to_left), (1, right, to_right)):
+            sent[sub].wait_recv()
+            staging[c, h, sub] = (
+                landing[c, h, sub].astype(F32) + view(sub, at)[...].astype(F32)
+            ).astype(BF16)
+            joined.append(copies.start(staging.at[c, h, sub], landing.at[c, h, 4 + sub], to))
+        return joined
+
+    def total(c, h, axis, view, landing, sent, joined, sub):
+        me = near[axis][0]
+        sent[2 + sub].wait_recv()
+        joined[sub].wait_recv()
+        return (
+            view(sub, me)[...].astype(F32)
+            + landing[c, h, 2 + sub].astype(F32)
+            + landing[c, h, 4 + sub].astype(F32)
+        ).astype(BF16)
+
+    sent1, joined1, sent2, joined2 = {}, {}, {}, {}
+
+    def send_part(c):
+        for h in range(2):
+            sent1[c, h] = scatter(c, h, second[h], functools.partial(piece, c, h), in1)
+
+    def join_part(c):
+        for h in range(2):
+            view = functools.partial(piece, c, h)
+            joined1[c, h] = join(c, h, second[h], view, in1, comb1, sent1[c, h])
+
+    def middle(c, h, sub, at):
+        return mid.at[c, h, sub, at]
+
+    def send_mid(c):
+        for h in range(2):
+            view = functools.partial(piece, c, h)
+            for sub in range(2):
+                mid[c, h, sub] = total(
+                    c, h, second[h], view, in1, sent1[c, h], joined1[c, h], sub
+                )
+            view = functools.partial(middle, c, h)
+            sent2[c, h] = scatter(c, h, first[h], view, in2)
+
+    def join_mid(c):
+        for h in range(2):
+            view = functools.partial(middle, c, h)
+            joined2[c, h] = join(c, h, first[h], view, in2, comb2, sent2[c, h])
+
+    def settle_out(c):
+        for h in range(2):
+            view = functools.partial(middle, c, h)
+            for sub in range(2):
+                out[c, h, sub] = total(
+                    c, h, first[h], view, in2, sent2[c, h], joined2[c, h], sub
+                )
+
+    multiply_out(0)
+    send_part(0)
+    multiply_out(1)
+    send_part(1)
+    multiply_out(2)
+    send_part(2)
+    join_part(0)
+    join_part(1)
+    send_mid(0)
+    join_part(2)
+    join_mid(0)
+    send_mid(1)
+    settle_out(0)
+    join_mid(1)
+    send_mid(2)
+    settle_out(1)
+    join_mid(2)
+    settle_out(2)
+    copies.finish()
+
+
+def experts(slots, w_gate, w_up, w_down):
+    units, width = w_gate.shape
+    blocked = slots.reshape(SLOTS, CHUNKS, 2, 2, WIDTH).transpose(1, 2, 3, 0, 4)
+    count = CHUNKS * 2 * (8 + 12) + 3
+    whole = (CHUNKS, 2, 2, RING, RING, SLOTS, WIDTH)
+    produced = pl.pallas_call(
+        experts_kernel,
+        out_shape=jax.ShapeDtypeStruct(blocked.shape, BF16),
+        in_specs=[pl.BlockSpec(memory_space=pltpu.VMEM)] + [pl.BlockSpec(memory_space=pl.ANY)] * 3,
+        out_specs=pl.BlockSpec(memory_space=pltpu.VMEM),
+        scratch_shapes=[
+            pltpu.VMEM(whole, BF16),
+            pltpu.VMEM((4 * units, width), BF16),
+            pltpu.VMEM((2 * units, width), BF16),
+            pltpu.VMEM((2, 4 * units, 256), F32),
+            pltpu.VMEM((RING * RING * SLOTS, 2 * units), BF16),
+            pltpu.VMEM(whole, BF16),
+            pltpu.VMEM((CHUNKS, 2, 6, RING, SLOTS, WIDTH), BF16),
+            pltpu.VMEM((CHUNKS, 2, 2, RING, SLOTS, WIDTH), BF16),
+            pltpu.VMEM((CHUNKS, 2, 2, RING, SLOTS, WIDTH), BF16),
+            pltpu.VMEM((CHUNKS, 2, 6, SLOTS, WIDTH), BF16),
+            pltpu.VMEM((CHUNKS, 2, 2, SLOTS, WIDTH), BF16),
+            pltpu.SemaphoreType.DMA((count,)),
+            pltpu.SemaphoreType.DMA((count,)),
+            pltpu.SemaphoreType.DMA((2 * CHUNKS + 3,)),
+        ],
+        compiler_params=pltpu.CompilerParams(
+            collective_id=3, has_side_effects=True, vmem_limit_bytes=64000 * 1024
+        ),
+        name="experts",
+    )(blocked, w_gate, w_up, w_down)
+    return produced.transpose(3, 0, 1, 2, 4).reshape(SLOTS, width)
 
 
 def body(
@@ -124,13 +433,7 @@
     ).astype(jnp.bfloat16)
     mine = lax.all_to_all(outgoing, "exp", 0, 0, tiled=True)
     mine = mine.reshape(group_count * capacity, -1)
-    gathered = lax.all_gather(mine, "ctx", axis=0, tiled=True)
-    produced = lax.psum_scatter(
-        expert_part(gathered, w_gate[0], w_up[0], w_down[0]).astype(jnp.bfloat16),
-        "ctx",
-        scatter_dimension=0,
-        tiled=True,
-    )
+    produced = experts(mine, w_gate[0], w_up[0], w_down[0])
     produced = produced.reshape(group_count, capacity, -1)
     returned = lax.all_to_all(produced, "exp", 0, 0, tiled=True)
     for column in range(2):

time: 363 us -> 251 us (0.69)
  waiting for transfers between devices: 258 us -> 107 us
  Pallas kernels: 0 us -> 88.4 us
  matrix products: 52.1 us -> 19.3 us
  blocking collectives: 11.5 us -> 0 us
  other arithmetic: 15.3 us -> 8.33 us
    reduce_scatter x1 -> x0, waiting for transfers between devices: 103 us -> none  [body(): lax.psum_scatter(expert_part(gathered, w_gate[0], w_up[0], w_down[0]).ast...]
    pallas_call x0 -> x1, Pallas kernels: none -> 88.4 us  [experts(): pl.pallas_call(experts_kernel, out_shape=jax.ShapeDtypeStruct(blocked.sha...]
    all_gather x1 -> x0, waiting for transfers between devices: 62.3 us -> none  [body(): gathered = lax.all_gather(mine, 'ctx', axis=0, tiled=True)]
    dot_general x2 -> x0, matrix products: 28.1 us -> none  [the longest x1 17.6 us: expert_part(): return jnp.dot(activated, down_rows, preferred_element_type=jnp.float32)]
    all_to_all x1 -> x0, blocking collectives: 11.5 us -> none  [body(): mine = lax.all_to_all(outgoing, 'exp', 0, 0, tiled=True)]
    all_to_all x0 -> x1, waiting for transfers between devices: none -> 8.08 us  [body(): mine = lax.all_to_all(outgoing, 'exp', 0, 0, tiled=True)]
    all_gather x1, waiting for transfers between devices: 48.4 us -> 54.7 us  [earlier_states(): lax.all_gather(update.astype(jnp.bfloat16), 'ctx').astype(jnp.float32)]
    all_to_all x0 -> x1, starting transfers between devices: none -> 3.64 us  [body(): mine = lax.all_to_all(outgoing, 'exp', 0, 0, tiled=True)]
  transfers between devices with their start and end apart: 5 -> 4, of which waited for: 5 -> 4; matrix products, arithmetic and copies ran while one was open for 2% -> 0% of each run, Pallas kernels for 0% -> 0%
where the time goes in v2:
time: 251 us; the launch traced here: 250 us
  waiting for transfers between devices  107 us (43%)
  Pallas kernels  88.4 us (35%)
  matrix products  19.3 us (8%)
  between operations  13.7 us (5%)
  other arithmetic  8.33 us (3%)
  starting transfers between devices  7.14 us (3%)
  local copies, waits for them, and re-layouts  5.93 us (2%)
    pallas_call x1, Pallas kernels, experts(): pl.pallas_call(experts_kernel, out_shape=jax.ShapeDtypeStruct(blocked.sha...  88.4 us
    all_gather x1, waiting for transfers between devices, earlier_states(): lax.all_gather(update.astype(jnp.bfloat16), 'ctx').astype(jnp.float32)  54.7 us
    reduce_scatter x1, waiting for transfers between devices, body(): lax.psum_scatter(projected.astype(jnp.bfloat16), 'exp', scatter_dimension...  37.1 us
    dot_general x1, matrix products, body(): projected = jnp.dot(settled, out_proj, preferred_element_type=jnp.float32)  9.51 us
    all_to_all x1, waiting for transfers between devices, body(): mine = lax.all_to_all(outgoing, 'exp', 0, 0, tiled=True)  8.08 us
    all_to_all x1, waiting for transfers between devices, body(): returned = lax.all_to_all(produced, 'exp', 0, 0, tiled=True)  7.32 us
    reduce_sum x1, other arithmetic, earlier_states(): return jnp.sum(everything * factors[:, :, None, None], axis=0)  5.1 us
  transfers between devices with their start and end apart: 4, of which 4 were waited for; matrix products, arithmetic and copies ran while one was open for 0% of the time, Pallas kernels for 0%

profile of v2, /device:TPU:0, one launch (start us, length us, event | category | flops | bytes accessed | tf_op | source)
XLA Modules:
  0.0 250.0 jit_solution(10544728077207375255)
XLA Ops:
  6.5 0.8 broadcast_multiply_fusion
  7.3 1.2 copy.38
  8.6 2.0 convolution_convert_fusion.2
  10.8 0.3 add_divide_fusion
  11.1 0.3 copy.34
  11.7 54.7 %all-gather.3.cloned.1.call-done = bf16[256,128,128]{2,1,0:T(8,128)(2,1)} async-done(((bf16[8,128,128]{2,1,0:T(8,128)(2,1)}), bf16[256,128,128]{2,1,0:T(8,128)(2,1)}) %all-gather.3.cloned.1.call-update) | async-done | bytes 8388624 | tf_op jit(solution)/shard_map/all_gather | solution.py:15
  66.3 5.1 %fusion = f32[8,128,128]{2,1,0:T(8,128)S(1)} fusion(bf16[32,8,128,128]{3,2,1,0:T(8,128)(2,1)} %bitcast.81, f32[32,8]{1,0:T(8,128)S(1)} %exponential_select_fusion), kind=kLoop, calls=%fused_computation.1 | loop fusion | flops 12451840 | bytes 8913920 | tf_op jit(solution)/shard_map/reduce_sum | solution.py:22
  71.5 2.4 convolution_bitcast_fusion.2
  73.8 2.3 multiply_reduce_fusion.1
  76.4 9.5 %convolution_convert_fusion = bf16[256,6144]{1,0:T(8,128)(2,1)} fusion(bf16[256,1024]{0,1:T(8,128)(2,1)S(1)} %bitcast.86, bf16[1024,6144]{1,0:T(8,128)(2,1)} %param.20), kind=kOutput, calls=%fused_computation.2 | convolution fusion | flops 3222798336 | bytes 16252928 | tf_op jit(solution)/shard_map/dot_general | solution.py:422
  86.0 0.6 copy-done.7
  86.9 37.1 %reduce-scatter.2.cloned.1.call-done = bf16[64,6144]{1,0:T(8,128)(2,1)} async-done(((bf16[256,6144]{1,0:T(8,128)(2,1)}), bf16[64,6144]{1,0:T(8,128)(2,1)}) %reduce-scatter.2.cloned.1.call-update) | async-done | bytes 786448 | tf_op jit(solution)/shard_map/reduce_scatter | solution.py:423
  124.0 1.6 multiply_reduce_fusion
  125.6 1.2 convolution_convert_fusion.1
  126.7 3.6 %all-to-all-start = ((bf16[4,8,6144]{2,1,0:T(8,128)(2,1)}), bf16[4,8,6144]{2,1,0:T(8,128)(2,1)S(1)}, u32[]{:S(2)}, u32[]{:S(2)}) async-start(bf16[4,8,6144]{2,1,0:T(8,128)(2,1)} %convolution_convert_fusion.1), calls=%async_computation.1 | async-start | bytes 786432 | tf_op jit(solution)/shard_map/all_to_all | solution.py:434
  130.5 8.1 %all-to-all-done = bf16[4,8,6144]{2,1,0:T(8,128)(2,1)S(1)} async-done(((bf16[4,8,6144]{2,1,0:T(8,128)(2,1)}), bf16[4,8,6144]{2,1,0:T(8,128)(2,1)S(1)}, u32[]{:S(2)}, u32[]{:S(2)}) %all-to-all-start) | async-done | bytes 393248 | tf_op jit(solution)/shard_map/all_to_all | solution.py:434
  138.8 0.8 copy.63
  139.7 88.4 %experts.1 = bf16[3,2,2,32,512]{4,3,2,1,0:T(8,128)(2,1)} custom-call(bf16[3,2,2,32,512]{4,3,2,1,0:T(8,128)(2,1)} %bitcast.87, bf16[288,6144]{1,0:T(8,128)(2,1)} %bitcast.83, bf16[288,6144]{1,0:T(8,128)(2,1)} %bitcast.84, bf16[288,6144]{1,0:T(8,128)(2,1)} %bitcast.85), custom_call_target="tpu_custom_call" | custom-call | tf_op jit(solution)/shard_map/experts/pallas_call | solution.py:367
  228.1 1.4 copy.36
  229.5 1.0 reshape_reshape.7
  230.5 3.5 %all-to-all-start.1 = ((bf16[4,8,6144]{2,1,0:T(8,128)(2,1)}), bf16[4,8,6144]{2,1,0:T(8,128)(2,1)S(1)}, u32[]{:S(2)}, u32[]{:S(2)}) async-start(bf16[4,8,6144]{2,1,0:T(8,128)(2,1)} %reshape_reshape.7), calls=%async_computation.2 | async-start | bytes 786432 | tf_op jit(solution)/shard_map/all_to_all | solution.py:438
  234.0 7.3 %all-to-all-done.1 = bf16[4,8,6144]{2,1,0:T(8,128)(2,1)S(1)} async-done(((bf16[4,8,6144]{2,1,0:T(8,128)(2,1)}), bf16[4,8,6144]{2,1,0:T(8,128)(2,1)S(1)}, u32[]{:S(2)}, u32[]{:S(2)}) %all-to-all-start.1) | async-done | bytes 393248 | tf_op jit(solution)/shard_map/all_to_all | solution.py:438
  241.3 0.4 fusion.4
  241.8 1.4 fusion.5
  (40 shorter events, 1.3 us)
Async XLA Ops:
  6.5 64.9 %copy-start = (bf16[256,1024]{1,0:T(8,128)(2,1)S(1)}, bf16[256,1024]{1,0:T(8,128)(2,1)}, u32[]{:S(2)}) copy-start(bf16[256,1024]{1,0:T(8,128)(2,1)} %param.14) | copy-start | bytes 1572868
  6.5 4.2 %copy-start.4 = (bf16[256,1024]{1,0:T(8,128)(2,1)S(1)}, bf16[256,1024]{1,0:T(8,128)(2,1)}, u32[]{:S(2)}) copy-start(bf16[256,1024]{1,0:T(8,128)(2,1)} %param.17) | copy-start | bytes 1572868
  6.5 59.8 %all-gather.3.cloned.1.call-start = ((), (), s32[]{:S(2)}) async-start(), calls=%async_computation.4 | async-start | bytes 8650752 | tf_op jit(solution)/shard_map/all_gather | solution.py:15
  10.7 113.2 %reduce-scatter.2.cloned.1.call-start = ((), (), s32[]{:S(2)}) async-start(), calls=%async_computation.3 | async-start | bytes 3932160 | tf_op jit(solution)/shard_map/reduce_scatter | solution.py:423
  73.8 2.3 copy-start.6
  85.9 0.7 copy-start.7
  85.9 38.0 %copy-start.1 = (bf16[64,6144]{1,0:T(8,128)(2,1)S(1)}, bf16[64,6144]{1,0:T(8,128)(2,1)}, u32[]{:S(2)}) copy-start(bf16[64,6144]{1,0:T(8,128)(2,1)} %param.21) | copy-start | bytes 2359300
  85.9 39.6 %copy-start.5 = (f32[6144]{0:T(1024)S(1)}, f32[6144]{0:T(1024)}, u32[]{:S(2)}) copy-start(f32[6144]{0:T(1024)} %param.22) | copy-start | bytes 73732
  124.0 1.6 copy-start.2
  125.5 4.9 %copy-start.8 = (f32[256,2]{0,1:T(2,128)S(1)}, f32[256,2]{0,1:T(2,128)}, u32[]{:S(2)}) copy-start(f32[256,2]{0,1:T(2,128)} %param.24) | copy-start | bytes 6148
  126.7 11.8 %all-to-all-start = ((bf16[4,8,6144]{2,1,0:T(8,128)(2,1)}), bf16[4,8,6144]{2,1,0:T(8,128)(2,1)S(1)}, u32[]{:S(2)}, u32[]{:S(2)}) async-start(bf16[4,8,6144]{2,1,0:T(8,128)(2,1)} %convolution_convert_fusion.1), calls=%async_computation.1 | async-start | bytes 786432 | tf_op jit(solution)/shard_map/all_to_all | solution.py:434
  229.5 12.3 %copy-start.3 = (bf16[64,6144]{1,0:T(8,128)(2,1)S(1)}, bf16[64,6144]{1,0:T(8,128)(2,1)}, u32[]{:S(2)}) copy-start(bf16[64,6144]{1,0:T(8,128)(2,1)} %reduce-scatter.2.cloned.1.call-done) | copy-start | bytes 2359300
  230.5 10.8 %all-to-all-start.1 = ((bf16[4,8,6144]{2,1,0:T(8,128)(2,1)}), bf16[4,8,6144]{2,1,0:T(8,128)(2,1)S(1)}, u32[]{:S(2)}, u32[]{:S(2)}) async-start(bf16[4,8,6144]{2,1,0:T(8,128)(2,1)} %reshape_reshape.7), calls=%async_computation.2 | async-start | bytes 786432 | tf_op jit(solution)/shard_map/all_to_all | solution.py:438
Sparse Core Ops, SparseCore 0:
  10.8 55.4 all-gather.2
  86.1 37.8 reduce-scatter.1

commit v3 on v2

--- a/solution.py
+++ b/solution.py
@@ -8,56 +8,192 @@
 from jax.sharding import PartitionSpec as P
 
 EPSILON = 1e-06
-
-
-def earlier_states(update, decay_rates, row_count):
-    size, index = (lax.axis_size("ctx"), lax.axis_index("ctx"))
-    everything = lax.all_gather(update.astype(jnp.bfloat16), "ctx").astype(jnp.float32)
-    distance = (index - 1 - jnp.arange(size)).astype(jnp.float32)
-    factors = jnp.where(
-        distance[:, None] >= 0.0,
-        jnp.exp(-decay_rates[None, :] * row_count * jnp.maximum(distance, 0.0)[:, None]),
-        0.0,
-    )
-    return jnp.sum(everything * factors[:, :, None, None], axis=0)
-
-
-def span_local(queries, key_rows, value_rows, decay_exp):
+MESH = pl.DeviceIdType.MESH
+BF16 = jnp.bfloat16
+F32 = jnp.float32
+RING = 4
+CHUNKS = 3
+WIDTH = 512
+SLOTS = 32
+
+
+def attention_kernel(
+    decay_exp, queries_hbm, keys_hbm, values_hbm, gates_hbm, attn_gain, settled,
+    queries, key_rows, value_rows, gate_rows, update, gathered, prior, state, inner,
+    send_sems, recv_sems, send_sems2, recv_sems2, local_sems,
+):
+    index, owner = lax.axis_index("ctx"), lax.axis_index("exp")
+    size = gathered.shape[0]
+    head_count = decay_exp.shape[0]
     row_count = queries.shape[0]
+    head_width = queries.shape[1] // head_count
+
+    loads = []
+    for n, (source, target) in enumerate(
+        (
+            (keys_hbm, key_rows),
+            (values_hbm, value_rows),
+            (queries_hbm, queries),
+            (gates_hbm, gate_rows),
+        )
+    ):
+        loads.append(pltpu.make_async_copy(source, target, local_sems.at[2 + n]))
+        loads[n].start()
+    barrier = pltpu.get_barrier_semaphore()
+
+    def greet(step, carry):
+        other = lax.rem(index + step, size)
+        pl.semaphore_signal(barrier, inc=1, device_id=(other, owner), device_id_type=MESH)
+        return carry
+
+    lax.fori_loop(1, size, greet, 0)
+
+    def rate_of(head, shape):
+        exponent = jnp.full(shape, decay_exp[head].astype(F32), F32)
+        return jnp.exp2(-exponent)
+
+    def columns(head):
+        return slice(head * head_width, (head + 1) * head_width)
+
+    positions = lax.broadcasted_iota(jnp.int32, (row_count, head_width), 0).astype(F32)
+    loads[0].wait()
+    loads[1].wait()
+    for head in range(head_count):
+        rate = rate_of(head, (1, head_width))
+        tail = jnp.exp(-rate * (row_count - 1.0 - positions))
+        keyed = (key_rows[:, columns(head)].astype(F32) * tail).astype(BF16)
+        product = lax.dot_general(
+            keyed,
+            value_rows[:, columns(head)],
+            (((0,), (0,)), ((), ())),
+            preferred_element_type=F32,
+        )
+        parts = size // head_count
+        update[head * parts : (head + 1) * parts] = product.astype(BF16).reshape(
+            parts, head_width // parts, head_width
+        )
+    pl.semaphore_wait(barrier, size - 1)
+
+    def exchange(source, target, send, recv):
+        def copy(step):
+            other = lax.rem(index + step, size)
+            return pltpu.make_async_remote_copy(
+                src_ref=source.at[other],
+                dst_ref=target.at[index],
+                send_sem=send.at[step - 1],
+                recv_sem=recv.at[step - 1],
+                device_id=(other, owner),
+                device_id_type=MESH,
+            )
+
+        def start(step, carry):
+            copy(step).start()
+            return carry
+
+        def arrive(step, carry):
+            copy(step).wait_recv()
+            return carry
+
+        def leave(step, carry):
+            copy(step).wait_send()
+            return carry
+
+        return (
+            lambda: lax.fori_loop(1, size, start, 0),
+            lambda: lax.fori_loop(1, size, arrive, 0),
+            lambda: lax.fori_loop(1, size, leave, 0),
+        )
+
+    start, arrive, leave = exchange(update, gathered, send_sems, recv_sems)
+    start()
+    kept = pltpu.make_async_copy(update.at[index], gathered.at[index], local_sems.at[0])
+    kept.start()
+
+    def inside(head):
+        rate = rate_of(head, (1, row_count))
+        row = lax.broadcasted_iota(jnp.int32, (row_count, row_count), 0)
+        column = lax.broadcasted_iota(jnp.int32, (row_count, row_count), 1)
+        offset = (row - column).astype(F32)
+        damping = jnp.where(offset >= 0.0, jnp.exp(-rate * jnp.maximum(offset, 0.0)), 0.0)
+        scores = lax.dot_general(
+            queries[:, columns(head)],
+            key_rows[:, columns(head)],
+            (((1,), (1,)), ((), ())),
+            preferred_element_type=F32,
+        )
+        mixing = (scores * damping).astype(BF16)
+        inner[head] = jnp.dot(mixing, value_rows[:, columns(head)], preferred_element_type=F32)
+
+    loads[2].wait()
+    loads[3].wait()
+    for head in range(head_count // 2):
+        inside(head)
+    kept.wait()
+    arrive()
+    mine = index // (size // head_count)
+    carry_decay = jnp.exp(-rate_of(mine, (1, head_width)) * float(row_count))
+    running = jnp.zeros(gathered.shape[1:], F32)
+    for block in range(size):
+        prior[block] = running.astype(BF16)
+        if block + 1 < size:
+            running = carry_decay * running + gathered[block].astype(F32)
+    start2, arrive2, leave2 = exchange(prior, state, send_sems2, recv_sems2)
+    start2()
+    kept2 = pltpu.make_async_copy(prior.at[index], state.at[index], local_sems.at[1])
+    kept2.start()
+    for head in range(head_count // 2, head_count):
+        inside(head)
+    leave()
+    kept2.wait()
+    arrive2()
+    for head in range(head_count):
+        rate = rate_of(head, (1, head_width))
+        parts = size // head_count
+        held = state[head * parts : (head + 1) * parts].reshape(head_width, head_width)
+        reached = jnp.dot(queries[:, columns(head)], held, preferred_element_type=F32)
+        mixed = inner[head] + reached * jnp.exp(-rate * (positions + 1.0))
+        mean_square = jnp.mean(mixed * mixed, axis=1, keepdims=True)
+        normed = mixed * lax.rsqrt(mean_square + EPSILON)
+        gate = gate_rows[:, columns(head)].astype(F32)
+        value = normed * attn_gain[:, columns(head)] * (1.0 / (1.0 + jnp.exp(-gate)))
+        settled[:, columns(head)] = value.astype(BF16)
+    leave2()
+
+
+def attention(queries, key_rows, value_rows, gate_rows, decay_exp, attn_gain):
+    row_count, width = queries.shape
     head_count = decay_exp.shape[0]
-    head_width = queries.shape[1] // head_count
-    query_heads = queries.reshape(row_count, head_count, head_width)
-    key_heads = key_rows.reshape(row_count, head_count, head_width)
-    value_heads = value_rows.reshape(row_count, head_count, head_width)
-    decay_rates = jnp.exp2(-decay_exp.astype(jnp.float32))
-    positions = jnp.arange(row_count, dtype=jnp.float32)
-    offsets = positions[:, None] - positions[None, :]
-    damping = jnp.where(
-        offsets[None] >= 0.0,
-        jnp.exp(-decay_rates[:, None, None] * jnp.maximum(offsets, 0.0)[None]),
-        0.0,
-    )
-    scores = jnp.einsum("thd,shd->hts", query_heads, key_heads, preferred_element_type=jnp.float32)
-    mixing = (scores * damping).astype(jnp.bfloat16)
-    inner_part = jnp.einsum("hts,shd->thd", mixing, value_heads, preferred_element_type=jnp.float32)
-    tail_decay = jnp.exp(-decay_rates[None, :] * (row_count - 1.0 - positions)[:, None])
-    keyed_rows = (key_heads.astype(jnp.float32) * tail_decay[:, :, None]).astype(jnp.bfloat16)
-    update = jnp.einsum("shd,she->hde", keyed_rows, value_heads, preferred_element_type=jnp.float32)
-    lead_decay = jnp.exp(-decay_rates[None, :] * (positions + 1.0)[:, None])
-    leading = query_heads.astype(jnp.float32) * lead_decay[:, :, None]
-    return (inner_part, leading, update, decay_rates)
-
-
-def settle(inner_part, leading, prior_state, gate_rows, attn_gain):
-    outer_part = jnp.einsum("thd,hde->the", leading, prior_state, precision=lax.Precision.HIGHEST)
-    mixed_heads = inner_part + outer_part
-    row_count, head_count, head_width = mixed_heads.shape
-    mean_square = jnp.mean(mixed_heads * mixed_heads, axis=2, keepdims=True)
-    normed_heads = mixed_heads * lax.rsqrt(mean_square + EPSILON)
-    gain_heads = attn_gain.reshape(head_count, head_width)
-    gate_heads = gate_rows.reshape(row_count, head_count, head_width).astype(jnp.float32)
-    settled = (normed_heads * gain_heads * jax.nn.sigmoid(gate_heads)).astype(jnp.bfloat16)
-    return settled.reshape(row_count, head_count * head_width)
+    head_width = width // head_count
+    size = lax.axis_size("ctx")
+    shares = (size, head_count * head_width // size, head_width)
+    return pl.pallas_call(
+        attention_kernel,
+        out_shape=jax.ShapeDtypeStruct(queries.shape, BF16),
+        in_specs=[pl.BlockSpec(memory_space=pltpu.SMEM)]
+        + [pl.BlockSpec(memory_space=pltpu.HBM)] * 4
+        + [pl.BlockSpec(memory_space=pltpu.VMEM)],
+        out_specs=pl.BlockSpec(memory_space=pltpu.VMEM),
+        scratch_shapes=[
+            pltpu.VMEM(queries.shape, BF16),
+            pltpu.VMEM(queries.shape, BF16),
+            pltpu.VMEM(queries.shape, BF16),
+            pltpu.VMEM(queries.shape, BF16),
+            pltpu.VMEM(shares, BF16),
+            pltpu.VMEM(shares, BF16),
+            pltpu.VMEM(shares, BF16),
+            pltpu.VMEM(shares, BF16),
+            pltpu.VMEM((head_count, row_count, head_width), F32),
+            pltpu.SemaphoreType.DMA((size - 1,)),
+            pltpu.SemaphoreType.DMA((size - 1,)),
+            pltpu.SemaphoreType.DMA((size - 1,)),
+            pltpu.SemaphoreType.DMA((size - 1,)),
+            pltpu.SemaphoreType.DMA((6,)),
+        ],
+        compiler_params=pltpu.CompilerParams(
+            collective_id=1, has_side_effects=True, vmem_limit_bytes=16000 * 1024
+        ),
+        name="attention",
+    )(decay_exp, queries, key_rows, value_rows, gate_rows, attn_gain.reshape(1, width))
 
 
 def token_norm(hidden, norm_gain):
@@ -74,15 +210,6 @@
     slot_rank = jnp.dot(picked.astype(jnp.float32), upto.astype(jnp.float32)) - 1.0
     slot_ids = jnp.arange(capacity, dtype=jnp.float32)
     return picked[:, None, :] & (slot_rank[:, None, :] == slot_ids[None, :, None])
-
-
-MESH = pl.DeviceIdType.MESH
-BF16 = jnp.bfloat16
-F32 = jnp.float32
-RING = 4
-CHUNKS = 3
-WIDTH = 512
-SLOTS = 32
 
 
 def place(index):
@@ -409,12 +536,8 @@
     w_up,
     w_down,
 ):
-    inner_part, leading, update, decay_rates = span_local(
-        queries, key_rows, value_rows, decay_exp
-    )
+    settled = attention(queries, key_rows, value_rows, gate_rows, decay_exp, attn_gain)
     span_rows = queries.shape[0]
-    prior_state = earlier_states(update, decay_rates, span_rows)
-    settled = settle(inner_part, leading, prior_state, gate_rows, attn_gain)
     group_count = lax.axis_size("exp")
     group_rows = span_rows // group_count
     first_mine = lax.axis_index("exp") * group_rows

time: 251 us -> 207 us (0.82)
  waiting for transfers between devices: 107 us -> 52.3 us
  Pallas kernels: 88.4 us -> 110 us
  matrix products: 19.3 us -> 12.5 us
  other arithmetic: 8.33 us -> 1.66 us
  local copies, waits for them, and re-layouts: 5.93 us -> 9.25 us
    all_gather x1 -> x0, waiting for transfers between devices: 54.7 us -> none  [earlier_states(): lax.all_gather(update.astype(jnp.bfloat16), 'ctx').astype(jnp.float32)]
    pallas_call x0 -> x1, Pallas kernels: none -> 21.7 us  [attention(): pl.pallas_call(attention_kernel, out_shape=jax.ShapeDtypeStruct(queries.s...]
    dot_general x3 -> x0, matrix products: 6.72 us -> none  [the longest x1 2.37 us: settle(): jnp.einsum('thd,hde->the', leading, prior_state, precision=lax.Precision....]
    reduce_sum x1 -> x0, other arithmetic: 5.1 us -> none  [earlier_states(): return jnp.sum(everything * factors[:, :, None, None], axis=0)]
    unnamed x18 -> x24, local copies, waits for them, and re-layouts: 0.66 us -> 5.54 us
  transfers between devices with their start and end apart: 4 -> 3, of which waited for: 4 -> 3; matrix products, arithmetic and copies ran while one was open for 0% -> 0% of each run, Pallas kernels for 0% -> 0%
where the time goes in v3:
time: 207 us
  Pallas kernels  110 us (53%)
  waiting for transfers between devices  52.3 us (25%)
  between operations  13.5 us (7%)
  matrix products  12.5 us (6%)
  local copies, waits for them, and re-layouts  9.25 us (4%)
  starting transfers between devices  7.1 us (3%)
    pallas_call x1, Pallas kernels, experts(): pl.pallas_call(experts_kernel, out_shape=jax.ShapeDtypeStruct(blocked.sha...  88.5 us
    reduce_scatter x1, waiting for transfers between devices, body(): lax.psum_scatter(projected.astype(jnp.bfloat16), 'exp', scatter_dimension...  36.8 us
    pallas_call x1, Pallas kernels, attention(): pl.pallas_call(attention_kernel, out_shape=jax.ShapeDtypeStruct(queries.s...  21.7 us
    dot_general x1, matrix products, body(): projected = jnp.dot(settled, out_proj, preferred_element_type=jnp.float32)  9.39 us
    all_to_all x1, waiting for transfers between devices, body(): mine = lax.all_to_all(outgoing, 'exp', 0, 0, tiled=True)  8.12 us
    all_to_all x1, waiting for transfers between devices, body(): returned = lax.all_to_all(produced, 'exp', 0, 0, tiled=True)  7.32 us
    unnamed x24, local copies, waits for them, and re-layouts  5.54 us
  transfers between devices with their start and end apart: 3, of which 3 were waited for; matrix products, arithmetic and copies ran while one was open for 0% of the time, Pallas kernels for 0%

profile of v3, /device:TPU:0, one launch (start us, length us, event | category | flops | bytes accessed | tf_op | source)
XLA Modules:
  0.0 206.5 jit_solution(12000948280555088063)
XLA Ops:
  6.5 1.1 copy-done.1
  7.6 1.0 copy-done.2
  8.6 1.0 copy-done.3
  9.7 1.0 copy-done.4
  10.7 0.7 copy-done.5
  11.4 0.7 copy-done.6
  12.1 21.7 %attention.1 = bf16[256,1024]{1,0:T(8,128)(2,1)S(1)} custom-call(s32[8]{0:T(128)S(1)} %copy-done.6, bf16[256,1024]{1,0:T(8,128)(2,1)S(1)} %copy-done.1, bf16[256,1024]{1,0:T(8,128)(2,1)S(1)} %copy-done.2, bf16[256,1024]{1,0:T(8,128)(2,1)S(1)} %copy-done.3, bf16[256,1024]{1,0:T(8,128)(2,1)S(1)} %copy-done.4, f32[1,1024]{1,0:T(1,128)S(1)} %bitcast.36), custom_call_target="tpu_custom_call" | custom-call | tf_op jit(solution)/shard_map/attention/pallas_call | solution.py:169
  33.8 9.4 %convolution_convert_fusion = bf16[256,6144]{1,0:T(8,128)(2,1)} fusion(bf16[256,1024]{1,0:T(8,128)(2,1)S(1)} %attention.1, bf16[1024,6144]{1,0:T(8,128)(2,1)} %param.20), kind=kOutput, calls=%fused_computation | convolution fusion | flops 3222798336 | bytes 16252928 | tf_op jit(solution)/shard_map/dot_general | solution.py:545
  43.2 0.1 constant_dynamic-slice_fusion
  43.4 0.1 convolution_add_fusion
  43.5 36.8 %reduce-scatter.2.cloned.1.call-done = bf16[64,6144]{1,0:T(8,128)(2,1)} async-done(((bf16[256,6144]{1,0:T(8,128)(2,1)}), bf16[64,6144]{1,0:T(8,128)(2,1)}) %reduce-scatter.2.cloned.1.call-update) | async-done | bytes 786448 | tf_op jit(solution)/shard_map/reduce_scatter | solution.py:546
  80.4 1.6 multiply_reduce_fusion
  82.0 1.2 convolution_convert_fusion.1
  83.1 3.6 %all-to-all-start = ((bf16[4,8,6144]{2,1,0:T(8,128)(2,1)}), bf16[4,8,6144]{2,1,0:T(8,128)(2,1)S(1)}, u32[]{:S(2)}, u32[]{:S(2)}) async-start(bf16[4,8,6144]{2,1,0:T(8,128)(2,1)} %convolution_convert_fusion.1), calls=%async_computation.1 | async-start | bytes 786432 | tf_op jit(solution)/shard_map/all_to_all | solution.py:557
  86.9 8.1 %all-to-all-done = bf16[4,8,6144]{2,1,0:T(8,128)(2,1)S(1)} async-done(((bf16[4,8,6144]{2,1,0:T(8,128)(2,1)}), bf16[4,8,6144]{2,1,0:T(8,128)(2,1)S(1)}, u32[]{:S(2)}, u32[]{:S(2)}) %all-to-all-start) | async-done | bytes 393248 | tf_op jit(solution)/shard_map/all_to_all | solution.py:557
  95.0 0.3 reshape_reshape.6
  95.3 0.8 copy.18
  96.1 88.5 %experts.1 = bf16[3,2,2,32,512]{4,3,2,1,0:T(8,128)(2,1)} custom-call(bf16[3,2,2,32,512]{4,3,2,1,0:T(8,128)(2,1)} %bitcast.40, bf16[288,6144]{1,0:T(8,128)(2,1)} %bitcast.37, bf16[288,6144]{1,0:T(8,128)(2,1)} %bitcast.38, bf16[288,6144]{1,0:T(8,128)(2,1)} %bitcast.39), custom_call_target="tpu_custom_call" | custom-call | tf_op jit(solution)/shard_map/experts/pallas_call | solution.py:494
  184.6 1.4 copy.16
  186.0 1.0 reshape_reshape.7
  187.0 3.5 %all-to-all-start.1 = ((bf16[4,8,6144]{2,1,0:T(8,128)(2,1)}), bf16[4,8,6144]{2,1,0:T(8,128)(2,1)S(1)}, u32[]{:S(2)}, u32[]{:S(2)}) async-start(bf16[4,8,6144]{2,1,0:T(8,128)(2,1)} %reshape_reshape.7), calls=%async_computation.2 | async-start | bytes 786432 | tf_op jit(solution)/shard_map/all_to_all | solution.py:561
  190.5 7.3 %all-to-all-done.1 = bf16[4,8,6144]{2,1,0:T(8,128)(2,1)S(1)} async-done(((bf16[4,8,6144]{2,1,0:T(8,128)(2,1)}), bf16[4,8,6144]{2,1,0:T(8,128)(2,1)S(1)}, u32[]{:S(2)}, u32[]{:S(2)}) %all-to-all-start.1) | async-done | bytes 393248 | tf_op jit(solution)/shard_map/all_to_all | solution.py:561
  197.9 0.4 fusion.3
  198.3 1.4 fusion.4
  (27 shorter events, 0.3 us)
Async XLA Ops:
  6.5 36.7 %copy-start = (s32[256,2]{0,1:T(2,128)S(1)}, s32[256,2]{0,1:T(2,128)}, u32[]{:S(2)}) copy-start(s32[256,2]{0,1:T(2,128)} %param.23) | copy-start | bytes 6148
  6.5 73.8 %reduce-scatter.2.cloned.1.call-start = ((), (), s32[]{:S(2)}) async-start(), calls=%async_computation.3 | async-start | bytes 3932160 | tf_op jit(solution)/shard_map/reduce_scatter | solution.py:546
  6.5 1.1 copy-start.1
  7.6 1.0 copy-start.2
  8.6 1.0 copy-start.3
  9.7 1.0 copy-start.4
  10.7 0.7 copy-start.5
  11.4 0.7 copy-start.6
  43.2 37.2 %copy-start.7 = (bf16[64,6144]{1,0:T(8,128)(2,1)S(1)}, bf16[64,6144]{1,0:T(8,128)(2,1)}, u32[]{:S(2)}) copy-start(bf16[64,6144]{1,0:T(8,128)(2,1)} %param.21) | copy-start | bytes 2359300
  43.2 38.7 %copy-start.10 = (f32[6144]{0:T(1024)S(1)}, f32[6144]{0:T(1024)}, u32[]{:S(2)}) copy-start(f32[6144]{0:T(1024)} %param.22) | copy-start | bytes 73732
  80.3 1.6 copy-start.8
  81.9 4.9 %copy-start.11 = (f32[256,2]{0,1:T(2,128)S(1)}, f32[256,2]{0,1:T(2,128)}, u32[]{:S(2)}) copy-start(f32[256,2]{0,1:T(2,128)} %param.24) | copy-start | bytes 6148
  83.1 11.9 %all-to-all-start = ((bf16[4,8,6144]{2,1,0:T(8,128)(2,1)}), bf16[4,8,6144]{2,1,0:T(8,128)(2,1)S(1)}, u32[]{:S(2)}, u32[]{:S(2)}) async-start(bf16[4,8,6144]{2,1,0:T(8,128)(2,1)} %convolution_convert_fusion.1), calls=%async_computation.1 | async-start | bytes 786432 | tf_op jit(solution)/shard_map/all_to_all | solution.py:557
  186.0 12.3 %copy-start.9 = (bf16[64,6144]{1,0:T(8,128)(2,1)S(1)}, bf16[64,6144]{1,0:T(8,128)(2,1)}, u32[]{:S(2)}) copy-start(bf16[64,6144]{1,0:T(8,128)(2,1)} %reduce-scatter.2.cloned.1.call-done) | copy-start | bytes 2359300
  187.0 10.8 %all-to-all-start.1 = ((bf16[4,8,6144]{2,1,0:T(8,128)(2,1)}), bf16[4,8,6144]{2,1,0:T(8,128)(2,1)S(1)}, u32[]{:S(2)}, u32[]{:S(2)}) async-start(bf16[4,8,6144]{2,1,0:T(8,128)(2,1)} %reshape_reshape.7), calls=%async_computation.2 | async-start | bytes 786432 | tf_op jit(solution)/shard_map/all_to_all | solution.py:561
Sparse Core Ops, SparseCore 0:
  43.3 36.9 reduce-scatter.1

commit v4 on v3

v4 whole, which is shorter than its diff:
```python
import functools

import jax
import jax.numpy as jnp
from jax import lax
from jax.experimental import pallas as pl
from jax.experimental.pallas import tpu as pltpu
from jax.sharding import PartitionSpec as P

EPSILON = 1e-06
MESH = pl.DeviceIdType.MESH
BF16 = jnp.bfloat16
F32 = jnp.float32
RING = 4
CHUNKS = 6
WIDTH = 256
SLOTS = 32


def attention_kernel(
    decay_exp, queries_hbm, keys_hbm, values_hbm, gates_hbm, attn_gain, settled,
    queries, key_rows, value_rows, gate_rows, update, gathered, prior, state, inner,
    send_sems, recv_sems, send_sems2, recv_sems2, local_sems,
):
    index, owner = lax.axis_index("ctx"), lax.axis_index("exp")
    size = gathered.shape[0]
    head_count = decay_exp.shape[0]
    row_count = queries.shape[0]
    head_width = queries.shape[1] // head_count

    loads = []
    for n, (source, target) in enumerate(
        (
            (keys_hbm, key_rows),
            (values_hbm, value_rows),
            (queries_hbm, queries),
            (gates_hbm, gate_rows),
        )
    ):
        loads.append(pltpu.make_async_copy(source, target, local_sems.at[2 + n]))
        loads[n].start()
    barrier = pltpu.get_barrier_semaphore()

    def greet(step, carry):
        other = lax.rem(index + step, size)
        pl.semaphore_signal(barrier, inc=1, device_id=(other, owner), device_id_type=MESH)
        return carry

    lax.fori_loop(1, size, greet, 0)

    def rate_of(head, shape):
        exponent = jnp.full(shape, decay_exp[head].astype(F32), F32)
        return jnp.exp2(-exponent)

    def columns(head):
        return slice(head * head_width, (head + 1) * head_width)

    positions = lax.broadcasted_iota(jnp.int32, (row_count, head_width), 0).astype(F32)
    loads[0].wait()
    loads[1].wait()
    for head in range(head_count):
        rate = rate_of(head, (1, head_width))
        tail = jnp.exp(-rate * (row_count - 1.0 - positions))
        keyed = (key_rows[:, columns(head)].astype(F32) * tail).astype(BF16)
        product = lax.dot_general(
            keyed,
            value_rows[:, columns(head)],
            (((0,), (0,)), ((), ())),
            preferred_element_type=F32,
        )
        parts = size // head_count
        update[head * parts : (head + 1) * parts] = product.astype(BF16).reshape(
            parts, head_width // parts, head_width
        )
    pl.semaphore_wait(barrier, size - 1)

    def exchange(source, target, send, recv):
        def copy(step):
            other = lax.rem(index + step, size)
            return pltpu.make_async_remote_copy(
                src_ref=source.at[other],
                dst_ref=target.at[index],
                send_sem=send.at[step - 1],
                recv_sem=recv.at[step - 1],
                device_id=(other, owner),
                device_id_type=MESH,
            )

        def start(step, carry):
            copy(step).start()
            return carry

        def arrive(step, carry):
            copy(step).wait_recv()
            return carry

        def leave(step, carry):
            copy(step).wait_send()
            return carry

        return (
            lambda: lax.fori_loop(1, size, start, 0),
            lambda: lax.fori_loop(1, size, arrive, 0),
            lambda: lax.fori_loop(1, size, leave, 0),
        )

    start, arrive, leave = exchange(update, gathered, send_sems, recv_sems)
    start()
    kept = pltpu.make_async_copy(update.at[index], gathered.at[index], local_sems.at[0])
    kept.start()

    def inside(head):
        rate = rate_of(head, (1, row_count))
        row = lax.broadcasted_iota(jnp.int32, (row_count, row_count), 0)
        column = lax.broadcasted_iota(jnp.int32, (row_count, row_count), 1)
        offset = (row - column).astype(F32)
        damping = jnp.where(offset >= 0.0, jnp.exp(-rate * jnp.maximum(offset, 0.0)), 0.0)
        scores = lax.dot_general(
            queries[:, columns(head)],
            key_rows[:, columns(head)],
            (((1,), (1,)), ((), ())),
            preferred_element_type=F32,
        )
        mixing = (scores * damping).astype(BF16)
        inner[head] = jnp.dot(mixing, value_rows[:, columns(head)], preferred_element_type=F32)

    loads[2].wait()
    loads[3].wait()
    for head in range(head_count // 2):
        inside(head)
    kept.wait()
    arrive()
    mine = index // (size // head_count)
    carry_decay = jnp.exp(-rate_of(mine, (1, head_width)) * float(row_count))
    running = jnp.zeros(gathered.shape[1:], F32)
    for block in range(size):
        prior[block] = running.astype(BF16)
        if block + 1 < size:
            running = carry_decay * running + gathered[block].astype(F32)
    start2, arrive2, leave2 = exchange(prior, state, send_sems2, recv_sems2)
    start2()
    kept2 = pltpu.make_async_copy(prior.at[index], state.at[index], local_sems.at[1])
    kept2.start()
    for head in range(head_count // 2, head_count):
        inside(head)
    leave()
    kept2.wait()
    arrive2()
    for head in range(head_count):
        rate = rate_of(head, (1, head_width))
        parts = size // head_count
        held = state[head * parts : (head + 1) * parts].reshape(head_width, head_width)
        reached = jnp.dot(queries[:, columns(head)], held, preferred_element_type=F32)
        mixed = inner[head] + reached * jnp.exp(-rate * (positions + 1.0))
        mean_square = jnp.mean(mixed * mixed, axis=1, keepdims=True)
        normed = mixed * lax.rsqrt(mean_square + EPSILON)
        gate = gate_rows[:, columns(head)].astype(F32)
        value = normed * attn_gain[:, columns(head)] * (1.0 / (1.0 + jnp.exp(-gate)))
        settled[:, columns(head)] = value.astype(BF16)
    leave2()


def attention(queries, key_rows, value_rows, gate_rows, decay_exp, attn_gain):
    row_count, width = queries.shape
    head_count = decay_exp.shape[0]
    head_width = width // head_count
    size = lax.axis_size("ctx")
    shares = (size, head_count * head_width // size, head_width)
    return pl.pallas_call(
        attention_kernel,
        out_shape=jax.ShapeDtypeStruct(queries.shape, BF16),
        in_specs=[pl.BlockSpec(memory_space=pltpu.SMEM)]
        + [pl.BlockSpec(memory_space=pltpu.HBM)] * 4
        + [pl.BlockSpec(memory_space=pltpu.VMEM)],
        out_specs=pl.BlockSpec(memory_space=pltpu.VMEM),
        scratch_shapes=[
            pltpu.VMEM(queries.shape, BF16),
            pltpu.VMEM(queries.shape, BF16),
            pltpu.VMEM(queries.shape, BF16),
            pltpu.VMEM(queries.shape, BF16),
            pltpu.VMEM(shares, BF16),
            pltpu.VMEM(shares, BF16),
            pltpu.VMEM(shares, BF16),
            pltpu.VMEM(shares, BF16),
            pltpu.VMEM((head_count, row_count, head_width), F32),
            pltpu.SemaphoreType.DMA((size - 1,)),
            pltpu.SemaphoreType.DMA((size - 1,)),
            pltpu.SemaphoreType.DMA((size - 1,)),
            pltpu.SemaphoreType.DMA((size - 1,)),
            pltpu.SemaphoreType.DMA((6,)),
        ],
        compiler_params=pltpu.CompilerParams(
            collective_id=1, has_side_effects=True, vmem_limit_bytes=64000 * 1024
        ),
        name="attention",
    )(decay_exp, queries, key_rows, value_rows, gate_rows, attn_gain.reshape(1, width))


def slot_table(chosen_ids, expert_count, capacity):
    owners = jnp.arange(expert_count, dtype=jnp.int32)
    chosen = jnp.where(owners[:, None] % 2 == 0, chosen_ids[None, :, 0], chosen_ids[None, :, 1])
    picked = chosen == owners[:, None]
    row_count = chosen_ids.shape[0]
    upto = jnp.arange(row_count)[:, None] <= jnp.arange(row_count)[None, :]
    slot_rank = jnp.dot(picked.astype(jnp.float32), upto.astype(jnp.float32)) - 1.0
    slot_ids = jnp.arange(capacity, dtype=jnp.float32)
    return picked[:, None, :] & (slot_rank[:, None, :] == slot_ids[None, :, None])


def place(index):
    return index // 8, (index // 2) % 4, index % 2


class Copies:
    def __init__(self, send_sems, recv_sems):
        self.send_sems, self.recv_sems = send_sems, recv_sems
        self.count, self.waiting = 0, []

    def start(self, source, target, device):
        copy = pltpu.make_async_remote_copy(
            src_ref=source,
            dst_ref=target,
            send_sem=self.send_sems.at[self.count],
            recv_sem=self.recv_sems.at[self.count],
            device_id=device,
            device_id_type=MESH,
        )
        copy.start()
        self.count += 1
        self.waiting.append(copy)
        return copy

    def finish(self):
        for copy in self.waiting:
            copy.wait_send()
        self.waiting = []


def layer_kernel(
    settled, out_proj, residual, norm_gain, pick, fetch, shares, w_gate, w_up, w_down, out,
    proj_w, proj, in0, comb0, hidden, squares, outbox, inbox, scale_out, scale_in, scales,
    rows, w_in, w_out, pre, act, in1, comb1, mid, in2, comb2, homebox, back,
    send_sems, recv_sems, local_sems,
):
    index, owner = lax.axis_index("ctx"), lax.axis_index("exp")
    z, x, core = place(index)
    part = rows

    def device(zz, xx):
        return (zz * 8 + xx * 2 + core, owner)

    def beside(at):
        return lax.rem(at + RING - 1, RING), lax.rem(at + 1, RING), lax.rem(at + 2, RING)

    x_left, x_right, x_far = beside(x)
    z_left, z_right, z_far = beside(z)
    y_left, y_right, y_far = beside(owner)
    partner = (index + 1 - 2 * core, owner)
    near = {
        "x": (x, x_left, x_right, device(z, x_left), device(z, x_right), x_far),
        "z": (z, z_left, z_right, device(z_left, x), device(z_right, x), z_far),
        "y": (owner, y_left, y_right, (index, y_left), (index, y_right), y_far),
    }
    column_peers = [lax.rem(owner + step, RING) for step in range(1, RING)]
    plane_peers = [
        device(lax.rem(z + dz, RING), lax.rem(x + dx, RING))
        for dz in range(RING)
        for dx in range(RING)
        if dz or dx
    ]
    barrier = pltpu.get_barrier_semaphore()
    greeted = [partner] + [(index, other) for other in column_peers] + plane_peers
    for other in greeted:
        pl.semaphore_signal(barrier, inc=1, device_id=other, device_id_type=MESH)
    copies = Copies(send_sems, recv_sems)
    local_count = [0]

    def local(source, target):
        copy = pltpu.make_async_copy(source, target, local_sems.at[local_count[0]])
        local_count[0] += 1
        copy.start()
        return copy

    units = w_gate.shape[0]
    piece_width = 4 * WIDTH
    half = 2 * WIDTH
    first, second = ("x", "z"), ("z", "x")
    both = slice(None)

    def scatter(axis, view, land):
        me, left, right, to_left, to_right, far = near[axis]
        return (
            copies.start(view(0, far), land(0), to_left),
            copies.start(view(1, far), land(1), to_right),
            copies.start(view(0, right), land(2), to_right),
            copies.start(view(1, left), land(3), to_left),
        )

    def join(axis, view, land, stage, sent):
        me, left, right, to_left, to_right, far = near[axis]
        joined = []
        for sub, at, to in ((0, left, to_left), (1, right, to_right)):
            sent[sub].wait_recv()
            stage(sub)[...] = (
                land(sub)[...].astype(F32) + view(sub, at)[...].astype(F32)
            ).astype(BF16)
            joined.append(copies.start(stage(sub), land(4 + sub), to))
        return joined

    def total(axis, view, land, sent, joined, sub):
        me = near[axis][0]
        sent[2 + sub].wait_recv()
        joined[sub].wait_recv()
        return (
            view(sub, me)[...].astype(F32)
            + land(2 + sub)[...].astype(F32)
            + land(4 + sub)[...].astype(F32)
        )

    loads = {}

    def load_proj(c):
        loads[c] = local(out_proj.at[:, pl.ds(c * piece_width, piece_width)], proj_w.at[c % 2])

    def project(c):
        loads[c].wait()
        for s in range(2):
            value = jnp.dot(
                settled[...],
                proj_w[c % 2, :, s * half : (s + 1) * half],
                preferred_element_type=F32,
            )
            proj[c, s] = value.astype(BF16).reshape(RING, -1, half)
        if c + 2 < CHUNKS:
            load_proj(c + 2)

    sent0, joined0, dispatched = {}, {}, {}

    def view0(c):
        return lambda sub, at: proj.at[c, sub, at]

    def land0(c):
        return lambda i: in0.at[c, i]

    def send_proj(c):
        sent0[c] = scatter("y", view0(c), land0(c))

    def join_proj(c):
        joined0[c] = join("y", view0(c), land0(c), lambda sub: comb0.at[c, sub], sent0[c])

    def exchange(box, landing):
        sent = [
            copies.start(box.at[other], landing.at[owner], (index, other))
            for other in column_peers
        ]
        return sent, local(box.at[owner], landing.at[owner])

    def arrive(exchanged):
        for copy in exchanged[0]:
            copy.wait_recv()
        exchanged[1].wait()

    def stacked(box, *place):
        return jnp.concatenate(
            [box[(*place[:1], e, *place[1:])].astype(F32) for e in range(RING)], axis=0
        )

    def dispatch(c):
        for s in range(2):
            columns = slice((c * 2 + s) * half, (c * 2 + s + 1) * half)
            value = total("y", view0(c), land0(c), sent0[c], joined0[c], s)
            value = value + residual[:, columns].astype(F32)
            hidden[c, s] = value
            square = value * value
            folded = square[:, :128]
            for lane in range(128, half, 128):
                folded = folded + square[:, lane : lane + 128]
            if c == 0 and s == 0:
                squares[...] = folded
            else:
                squares[...] = squares[...] + folded
            scaled = (value * norm_gain[:, columns]).astype(BF16)
            picked = jnp.dot(pick[...], scaled, preferred_element_type=F32)
            for e in range(RING):
                outbox[c, e, s] = picked[8 * e : 8 * e + 8].astype(BF16)
        dispatched[c] = exchange(outbox.at[c], inbox.at[c])

    def send_scales():
        mean_square = jnp.sum(squares[...], axis=1, keepdims=True) / (CHUNKS * piece_width)
        inverse = jnp.broadcast_to(lax.rsqrt(mean_square + EPSILON), squares.shape)
        picked = jnp.dot(
            pick[...].astype(F32),
            inverse,
            precision=lax.Precision.HIGHEST,
            preferred_element_type=F32,
        )
        for e in range(RING):
            scale_out[e] = picked[8 * e : 8 * e + 8]
        return exchange(scale_out, scale_in)

    def share_scales(exchanged):
        arrive(exchanged)
        mine = jnp.concatenate([scale_in[e] for e in range(RING)], axis=0)
        row = lax.broadcasted_iota(jnp.int32, (SLOTS, 128), 0)
        lane = lax.broadcasted_iota(jnp.int32, (SLOTS, 128), 1)
        line = jnp.sum(jnp.where(lane == x * SLOTS + row, mine, 0.0), axis=0, keepdims=True)
        scales[z, x] = jnp.broadcast_to(line, (8, 128))
        return [copies.start(scales.at[z, x], scales.at[z, x], other) for other in plane_peers]

    gather1, relay1, gather2, relay2 = {}, {}, {}, {}

    def line_of(c, h, stage, sub, at):
        axis = (first if stage == 1 else second)[h]
        if stage == 1:
            return rows.at[c, h, sub, at, x] if axis == "z" else rows.at[c, h, sub, z, at]
        return rows.at[c, h, sub, at] if axis == "z" else rows.at[c, h, sub, :, at]

    def spread(c, h, stage, started):
        me, left, right, to_left, to_right, far = near[(first if stage == 1 else second)[h]]
        mine = line_of(c, h, stage, both, me)
        started[c, h] = (copies.start(mine, mine, to_right), copies.start(mine, mine, to_left))

    def pass_on(c, h, stage, started, passed):
        me, left, right, to_left, to_right, far = near[(first if stage == 1 else second)[h]]
        from_left, from_right = started[c, h]
        from_left.wait_recv()
        source = line_of(c, h, stage, 0, left)
        one = copies.start(source, source, to_right)
        from_right.wait_recv()
        source = line_of(c, h, stage, 1, right)
        passed[c, h] = (one, copies.start(source, source, to_left))

    def gather_start(c):
        arrive(dispatched[c])
        for s in range(2):
            value = stacked(inbox, c, s).astype(BF16)
            for sub in range(2):
                rows[c, s, sub, z, x] = value[:, sub * WIDTH : (sub + 1) * WIDTH]
        for h in range(2):
            spread(c, h, 1, gather1)

    def gather_pass(c):
        for h in range(2):
            pass_on(c, h, 1, gather1, relay1)

    def gather_wide(c):
        for h in range(2):
            for copy in relay1[c, h]:
                copy.wait_recv()
            spread(c, h, 2, gather2)

    def gather_wide_pass(c):
        for h in range(2):
            pass_on(c, h, 2, gather2, relay2)

    weights = []

    def load_weights():
        for source, target, base in (
            (w_gate, w_in, 0),
            (w_up, w_in, 2 * units),
            (w_down, w_out, 0),
        ):
            kept = local(source, target.at[pl.ds(base, units)])
            sent = copies.start(source, target.at[pl.ds(base + units, units)], partner)
            weights.append((kept, sent))

    def multiply_in(c):
        for cc in (c, c + 1):
            for h in range(2):
                for copy in relay2[cc, h]:
                    copy.wait_recv()
        if c == 0:
            for n in range(2):
                weights[n][0].wait()
                weights[n][1].wait_recv()

        def tile(t, carry):
            total = None
            for cc in (c, c + 1):
                for h in range(2):
                    for sub in range(2):
                        block = rows[cc, h, sub, pl.ds(2 * t, 2)].reshape(256, WIDTH)
                        column = ((cc * 2 + h) * 2 + sub) * WIDTH
                        term = lax.dot_general(
                            w_in[:, column : column + WIDTH],
                            block,
                            (((1,), (1,)), ((), ())),
                            preferred_element_type=F32,
                        )
                        total = term if total is None else total + term
            pre[t] = total if c == 0 else pre[t] + total
            return carry

        lax.fori_loop(0, 2, tile, 0)

    def activate(t, carry):
        scale = jnp.concatenate(
            [jnp.sum(scales[2 * t + n], axis=0)[0:1] for n in range(2)], axis=1
        )
        gate = pre[t, : 2 * units] * scale
        up = pre[t, 2 * units :] * scale
        value = gate / (1.0 + jnp.exp(-gate)) * up
        act[pl.ds(pl.multiple_of(t * 256, 256), 256), :] = value.T.astype(BF16)
        return carry

    def multiply_out(c):
        def block(n, carry):
            column = pl.multiple_of((c * 4 + n) * WIDTH, WIDTH)
            value = jnp.dot(
                act[...], w_out[:, pl.ds(column, WIDTH)], preferred_element_type=F32
            )
            part[c, n // 2, n % 2] = value.astype(BF16).reshape(RING, RING, SLOTS, WIDTH)
            return carry

        lax.fori_loop(0, 4, block, 0)

    sent1, joined1, sent2, joined2, returned = {}, {}, {}, {}, {}

    def view1(c, h):
        if second[h] == "z":
            return lambda sub, at: part.at[c, h, sub, at]
        return lambda sub, at: part.at[c, h, sub, :, at]

    def view2(c, h):
        return lambda sub, at: mid.at[c, h, sub, at]

    def land1(c, h):
        return lambda i: in1.at[c, h, i]

    def land2(c, h):
        return lambda i: in2.at[c, h, i]

    def send_part(c):
        for h in range(2):
            sent1[c, h] = scatter(second[h], view1(c, h), land1(c, h))

    def join_part(c):
        for h in range(2):
            joined1[c, h] = join(
                second[h], view1(c, h), land1(c, h), lambda sub: comb1.at[c, h, sub], sent1[c, h]
            )

    def send_mid(c):
        for h in range(2):
            for sub in range(2):
                mid[c, h, sub] = total(
                    second[h], view1(c, h), land1(c, h), sent1[c, h], joined1[c, h], sub
                ).astype(BF16)
            sent2[c, h] = scatter(first[h], view2(c, h), land2(c, h))

    def join_mid(c):
        for h in range(2):
            joined2[c, h] = join(
                first[h], view2(c, h), land2(c, h), lambda sub: comb2.at[c, h, sub], sent2[c, h]
            )

    def send_home(c):
        for h in range(2):
            for sub in range(2):
                value = total(first[h], view2(c, h), land2(c, h), sent2[c, h], joined2[c, h], sub)
                for g in range(RING):
                    homebox[c, g, h, :, sub * WIDTH : (sub + 1) * WIDTH] = value[
                        8 * g : 8 * g + 8
                    ].astype(BF16)
        returned[c] = exchange(homebox.at[c], back.at[c])

    def finish(c):
        arrive(returned[c])
        for s in range(2):
            columns = slice((c * 2 + s) * half, (c * 2 + s + 1) * half)
            value = hidden[c, s]
            produced = stacked(back, c, s).astype(BF16)
            for column in range(2):
                fetched = jnp.dot(fetch[column], produced, preferred_element_type=F32)
                value = value + shares[:, column : column + 1] * fetched
            out[:, columns] = value.astype(BF16)

    load_proj(0)
    load_proj(1)
    project(0)
    pl.semaphore_wait(barrier, len(greeted))
    send_proj(0)
    scale_step = None
    for tick in range(1, CHUNKS + 6):
        if tick < CHUNKS:
            project(tick)
            send_proj(tick)
        if tick == 2:
            load_weights()
        if 0 <= tick - 4 < CHUNKS:
            gather_wide(tick - 4)
        if 0 <= tick - 3 < CHUNKS:
            gather_start(tick - 3)
        if 0 <= tick - 1 < CHUNKS:
            join_proj(tick - 1)
        if 0 <= tick - 3 < CHUNKS:
            gather_pass(tick - 3)
        if 0 <= tick - 2 < CHUNKS:
            dispatch(tick - 2)
            if tick - 2 == CHUNKS - 1:
                scale_step = send_scales()
        if 0 <= tick - 5 < CHUNKS:
            gather_wide_pass(tick - 5)
        if tick - 2 == CHUNKS:
            shared = share_scales(scale_step)
        done = tick - 6
        if 0 <= done < CHUNKS and done % 2 == 1 and done < CHUNKS - 1:
            multiply_in(done - 1)
    multiply_in(CHUNKS - 2)
    for copy in shared:
        copy.wait_recv()
    lax.fori_loop(0, 2, activate, 0)
    weights[2][0].wait()
    weights[2][1].wait_recv()
    copies.finish()
    for step in range(CHUNKS + 6):
        if step < CHUNKS:
            multiply_out(step)
            send_part(step)
        if 0 <= step - 2 < CHUNKS:
            join_part(step - 2)
        if 0 <= step - 3 < CHUNKS:
            send_mid(step - 3)
        if 0 <= step - 4 < CHUNKS:
            join_mid(step - 4)
        if 0 <= step - 5 < CHUNKS:
            send_home(step - 5)
        if 0 <= step - 6 < CHUNKS:
            finish(step - 6)
    copies.finish()


def layer_tail(settled, out_proj, residual, norm_gain, pick, fetch, shares, w_gate, w_up, w_down):
    units, width = w_gate.shape
    group_rows = residual.shape[0]
    depth = settled.shape[1]
    half = 2 * WIDTH
    count = CHUNKS * (6 + 3 + 3 + 16 + 24) + 3 + 15 + 3
    whole = (CHUNKS, 2, 2, RING, RING, SLOTS, WIDTH)
    box = (CHUNKS, RING, 2, SLOTS // RING, half)
    vmem = pl.BlockSpec(memory_space=pltpu.VMEM)
    anywhere = pl.BlockSpec(memory_space=pl.ANY)
    return pl.pallas_call(
        layer_kernel,
        out_shape=jax.ShapeDtypeStruct(residual.shape, BF16),
        in_specs=[vmem, anywhere, vmem, vmem, vmem, vmem, vmem] + [anywhere] * 3,
        out_specs=vmem,
        scratch_shapes=[
            pltpu.VMEM((2, depth, 4 * WIDTH), BF16),
            pltpu.VMEM((CHUNKS, 2, RING, group_rows, half), BF16),
            pltpu.VMEM((CHUNKS, 6, group_rows, half), BF16),
            pltpu.VMEM((CHUNKS, 2, group_rows, half), BF16),
            pltpu.VMEM((CHUNKS, 2, group_rows, half), F32),
            pltpu.VMEM((group_rows, 128), F32),
            pltpu.VMEM(box, BF16),
            pltpu.VMEM(box, BF16),
            pltpu.VMEM((RING, SLOTS // RING, 128), F32),
            pltpu.VMEM((RING, SLOTS // RING, 128), F32),
            pltpu.VMEM((RING, RING, 8, 128), F32),
            pltpu.VMEM(whole, BF16),
            pltpu.VMEM((4 * units, width), BF16),
            pltpu.VMEM((2 * units, width), BF16),
            pltpu.VMEM((2, 4 * units, 256), F32),
            pltpu.VMEM((RING * RING * SLOTS, 2 * units), BF16),
            pltpu.VMEM((CHUNKS, 2, 6, RING, SLOTS, WIDTH), BF16),
            pltpu.VMEM((CHUNKS, 2, 2, RING, SLOTS, WIDTH), BF16),
            pltpu.VMEM((CHUNKS, 2, 2, RING, SLOTS, WIDTH), BF16),
            pltpu.VMEM((CHUNKS, 2, 6, SLOTS, WIDTH), BF16),
            pltpu.VMEM((CHUNKS, 2, 2, SLOTS, WIDTH), BF16),
            pltpu.VMEM(box, BF16),
            pltpu.VMEM(box, BF16),
            pltpu.SemaphoreType.DMA((count,)),
            pltpu.SemaphoreType.DMA((count,)),
            pltpu.SemaphoreType.DMA((3 * CHUNKS + 4,)),
        ],
        compiler_params=pltpu.CompilerParams(
            collective_id=2, has_side_effects=True, vmem_limit_bytes=64000 * 1024
        ),
        name="layer_tail",
    )(
        settled, out_proj, residual, norm_gain.reshape(1, width), pick, fetch, shares,
        w_gate, w_up, w_down,
    )


def body(
    queries,
    key_rows,
    value_rows,
    gate_rows,
    decay_exp,
    attn_gain,
    out_proj,
    residual,
    norm_gain,
    routes,
    route_weights,
    w_gate,
    w_up,
    w_down,
):
    settled = attention(queries, key_rows, value_rows, gate_rows, decay_exp, attn_gain)
    span_rows = queries.shape[0]
    group_count = lax.axis_size("exp")
    group_rows = span_rows // group_count
    first_mine = lax.axis_index("exp") * group_rows
    capacity = group_rows // 8
    my_routes = lax.dynamic_slice_in_dim(routes, first_mine, group_rows, 0)
    my_weights = lax.dynamic_slice_in_dim(route_weights, first_mine, group_rows, 0)
    table = slot_table(my_routes, group_count, capacity)
    pick = table.reshape(group_count * capacity, group_rows)
    even = (jnp.arange(group_count * capacity) // capacity) % 2 == 0
    fetch = jnp.stack([pick.T & even, pick.T & ~even]).astype(BF16)
    return layer_tail(
        settled,
        out_proj,
        residual,
        norm_gain,
        pick.astype(BF16),
        fetch,
        my_weights,
        w_gate[0],
        w_up[0],
        w_down[0],
    )


def solution(mesh):
    in_specs = (
        P("ctx", "exp"),
        P("ctx", "exp"),
        P("ctx", "exp"),
        P("ctx", "exp"),
        P("exp"),
        P("exp"),
        P("exp", None),
        P(("ctx", "exp"), None),
        P(),
        P("ctx", None),
        P("ctx", None),
        P("exp", "ctx", None),
        P("exp", "ctx", None),
        P("exp", "ctx", None),
    )
    out_specs = P(("ctx", "exp"), None)
    return jax.shard_map(body, mesh=mesh, in_specs=in_specs, out_specs=out_specs, check_vma=False)
```

time: 207 us -> 163 us (0.79)
  waiting for transfers between devices: 52.3 us -> 0 us
  Pallas kernels: 110 us -> 157 us
  between operations: 13.5 us -> 0.05 us
  matrix products: 12.5 us -> 0.13 us
  starting transfers between devices: 7.1 us -> 0 us
  local copies, waits for them, and re-layouts: 9.25 us -> 5.23 us
    pallas_call x1, Pallas kernels: 88.5 us -> 134 us  [layer_tail(): pl.pallas_call(layer_kernel, out_shape=jax.ShapeDtypeStruct(residual.shap...]
    reduce_scatter x1 -> x0, waiting for transfers between devices: 36.8 us -> none  [body(): lax.psum_scatter(projected.astype(jnp.bfloat16), 'exp', scatter_dimension...]
    all_to_all x2 -> x0, waiting for transfers between devices: 15.4 us -> none  [the longest x1 8.12 us: body(): mine = lax.all_to_all(outgoing, 'exp', 0, 0, tiled=True)]
    dot_general x4 -> x0, matrix products: 12.4 us -> none  [the longest x1 9.39 us: body(): projected = jnp.dot(settled, out_proj, preferred_element_type=jnp.float32)]
    all_to_all x2 -> x0, starting transfers between devices: 7.1 us -> none  [the longest x1 3.64 us: body(): mine = lax.all_to_all(outgoing, 'exp', 0, 0, tiled=True)]
    another operation x3 -> x0, local copies, waits for them, and re-layouts: 2.13 us -> none  [the longest x2 1.1 us: experts(): blocked = slots.reshape(SLOTS, CHUNKS, 2, 2, WIDTH).transpose(1, 2, 3, 0, 4)]
    unnamed x24 -> x4, local copies, waits for them, and re-layouts: 5.54 us -> 3.45 us
  transfers between devices with their start and end apart: 3 -> 0, of which waited for: 3 -> 0; matrix products, arithmetic and copies ran while one was open for 0% -> 0% of each run, Pallas kernels for 0% -> 0%
where the time goes in v4:
time: 163 us
  Pallas kernels  157 us (96%)
  local copies, waits for them, and re-layouts  5.23 us (3%)
    pallas_call x1, Pallas kernels, layer_tail(): pl.pallas_call(layer_kernel, out_shape=jax.ShapeDtypeStruct(residual.shap...  134 us
    pallas_call x1, Pallas kernels, attention(): pl.pallas_call(attention_kernel, out_shape=jax.ShapeDtypeStruct(queries.s...  22.5 us
    unnamed x4, local copies, waits for them, and re-layouts  3.45 us

profile of v4, /device:TPU:0, one launch (start us, length us, event | category | flops | bytes accessed | tf_op | source)
XLA Modules:
  0.0 162.8 jit_solution(104182994642723482)
XLA Ops:
  0.0 0.0 copy-start
  0.0 0.7 copy-done
  0.7 0.1 constant_dynamic-slice_fusion.1
  0.8 0.1 iota_compare_fusion.2
  0.8 0.7 constant_dynamic-slice_fusion
  1.6 0.1 convolution_add_fusion
  1.7 0.1 eq.63
  1.8 0.1 copy.24
  1.9 0.1 copy.22
  2.1 0.7 copy.26.pick
  2.7 0.6 add_convert_fusion.fetch
  3.4 0.7 copy.27.shares
  4.1 22.5 %attention.1.settled = bf16[256,1024]{1,0:T(8,128)(2,1)} custom-call(s32[8]{0:T(128)} %decay_exp.1, bf16[256,1024]{1,0:T(8,128)(2,1)} %queries_hbm.1, bf16[256,1024]{1,0:T(8,128)(2,1)} %keys_hbm.1, bf16[256,1024]{1,0:T(8,128)(2,1)} %values_hbm.1, bf16[256,1024]{1,0:T(8,128)(2,1)} %gates_hbm.1, f32[1,1024]{1,0:T(1,128)} %bitcast.26), custom_call_target="tpu_custom_call" | custom-call | tf_op jit(solution)/shard_map/attention/pallas_call | solution.py:169
  26.6 134.1 %layer_tail.1 = bf16[64,6144]{1,0:T(8,128)(2,1)} custom-call(bf16[256,1024]{1,0:T(8,128)(2,1)} %attention.1.settled, bf16[1024,6144]{1,0:T(8,128)(2,1)} %out_proj.1, bf16[64,6144]{1,0:T(8,128)(2,1)} %residual.1, f32[1,6144]{1,0:T(1,128)} %bitcast.25, bf16[32,64]{1,0:T(8,128)(2,1)} %copy.26.pick, bf16[2,64,32]{2,1,0:T(8,128)(2,1)} %add_convert_fusion.fetch, ...), custom_call_target="tpu_custom_call" | custom-call | tf_op jit(solution)/shard_map/layer_tail/pallas_call | solution.py:644
  160.7 2.1 %copy.29 = bf16[64,6144]{1,0:T(8,128)(2,1)} copy(bf16[64,6144]{1,0:T(8,128)(2,1)} %layer_tail.1) | data formatting | bytes 1572864
  (8 shorter events, 0.1 us)
Async XLA Ops:
  0.0 0.7 copy-start

commit v5 on v4

--- a/solution.py
+++ b/solution.py
@@ -1,5 +1,3 @@
-import functools
-
 import jax
 import jax.numpy as jnp
 from jax import lax
@@ -17,8 +15,8 @@
 SLOTS = 32
 
 
-def attention_kernel(
-    decay_exp, queries_hbm, keys_hbm, values_hbm, gates_hbm, attn_gain, settled,
+def attend(
+    meet, decay_exp, queries_hbm, keys_hbm, values_hbm, gates_hbm, attn_gain, settled,
     queries, key_rows, value_rows, gate_rows, update, gathered, prior, state, inner,
     send_sems, recv_sems, send_sems2, recv_sems2, local_sems,
 ):
@@ -39,15 +37,6 @@
     ):
         loads.append(pltpu.make_async_copy(source, target, local_sems.at[2 + n]))
         loads[n].start()
-    barrier = pltpu.get_barrier_semaphore()
-
-    def greet(step, carry):
-        other = lax.rem(index + step, size)
-        pl.semaphore_signal(barrier, inc=1, device_id=(other, owner), device_id_type=MESH)
-        return carry
-
-    lax.fori_loop(1, size, greet, 0)
-
     def rate_of(head, shape):
         exponent = jnp.full(shape, decay_exp[head].astype(F32), F32)
         return jnp.exp2(-exponent)
@@ -72,7 +61,7 @@
         update[head * parts : (head + 1) * parts] = product.astype(BF16).reshape(
             parts, head_width // parts, head_width
         )
-    pl.semaphore_wait(barrier, size - 1)
+    meet()
 
     def exchange(source, target, send, recv):
         def copy(step):
@@ -160,53 +149,6 @@
     leave2()
 
 
-def attention(queries, key_rows, value_rows, gate_rows, decay_exp, attn_gain):
-    row_count, width = queries.shape
-    head_count = decay_exp.shape[0]
-    head_width = width // head_count
-    size = lax.axis_size("ctx")
-    shares = (size, head_count * head_width // size, head_width)
-    return pl.pallas_call(
-        attention_kernel,
-        out_shape=jax.ShapeDtypeStruct(queries.shape, BF16),
-        in_specs=[pl.BlockSpec(memory_space=pltpu.SMEM)]
-        + [pl.BlockSpec(memory_space=pltpu.HBM)] * 4
-        + [pl.BlockSpec(memory_space=pltpu.VMEM)],
-        out_specs=pl.BlockSpec(memory_space=pltpu.VMEM),
-        scratch_shapes=[
-            pltpu.VMEM(queries.shape, BF16),
-            pltpu.VMEM(queries.shape, BF16),
-            pltpu.VMEM(queries.shape, BF16),
-            pltpu.VMEM(queries.shape, BF16),
-            pltpu.VMEM(shares, BF16),
-            pltpu.VMEM(shares, BF16),
-            pltpu.VMEM(shares, BF16),
-            pltpu.VMEM(shares, BF16),
-            pltpu.VMEM((head_count, row_count, head_width), F32),
-            pltpu.SemaphoreType.DMA((size - 1,)),
-            pltpu.SemaphoreType.DMA((size - 1,)),
-            pltpu.SemaphoreType.DMA((size - 1,)),
-            pltpu.SemaphoreType.DMA((size - 1,)),
-            pltpu.SemaphoreType.DMA((6,)),
-        ],
-        compiler_params=pltpu.CompilerParams(
-            collective_id=1, has_side_effects=True, vmem_limit_bytes=64000 * 1024
-        ),
-        name="attention",
-    )(decay_exp, queries, key_rows, value_rows, gate_rows, attn_gain.reshape(1, width))
-
-
-def slot_table(chosen_ids, expert_count, capacity):
-    owners = jnp.arange(expert_count, dtype=jnp.int32)
-    chosen = jnp.where(owners[:, None] % 2 == 0, chosen_ids[None, :, 0], chosen_ids[None, :, 1])
-    picked = chosen == owners[:, None]
-    row_count = chosen_ids.shape[0]
-    upto = jnp.arange(row_count)[:, None] <= jnp.arange(row_count)[None, :]
-    slot_rank = jnp.dot(picked.astype(jnp.float32), upto.astype(jnp.float32)) - 1.0
-    slot_ids = jnp.arange(capacity, dtype=jnp.float32)
-    return picked[:, None, :] & (slot_rank[:, None, :] == slot_ids[None, :, None])
-
-
 def place(index):
     return index // 8, (index // 2) % 4, index % 2
 
@@ -237,7 +179,11 @@
 
 
 def layer_kernel(
-    settled, out_proj, residual, norm_gain, pick, fetch, shares, w_gate, w_up, w_down, out,
+    decay_exp, queries_hbm, keys_hbm, values_hbm, gates_hbm, attn_gain,
+    out_proj, residual_hbm, norm_gain, routes, route_weights, w_gate, w_up, w_down, out,
+    queries, key_rows, value_rows, gate_rows, update, gathered, prior, state, inner,
+    state_sems, state_sems2, state_sems3, state_sems4, span_sems,
+    settled, residual, pick, fetch, shares,
     proj_w, proj, in0, comb0, hidden, squares, outbox, inbox, scale_out, scale_in, scales,
     rows, w_in, w_out, pre, act, in1, comb1, mid, in2, comb2, homebox, back,
     send_sems, recv_sems, local_sems,
@@ -269,9 +215,16 @@
         if dz or dx
     ]
     barrier = pltpu.get_barrier_semaphore()
-    greeted = [partner] + [(index, other) for other in column_peers] + plane_peers
-    for other in greeted:
-        pl.semaphore_signal(barrier, inc=1, device_id=other, device_id_type=MESH)
+    size = gathered.shape[0]
+
+    def greet(step, carry):
+        other = lax.rem(index + step, size)
+        pl.semaphore_signal(barrier, inc=1, device_id=(other, owner), device_id_type=MESH)
+        return carry
+
+    lax.fori_loop(1, size, greet, 0)
+    for other in column_peers:
+        pl.semaphore_signal(barrier, inc=1, device_id=(index, other), device_id_type=MESH)
     copies = Copies(send_sems, recv_sems)
     local_count = [0]
 
@@ -316,6 +269,41 @@
             + land(2 + sub)[...].astype(F32)
             + land(4 + sub)[...].astype(F32)
         )
+
+    def tables():
+        group_rows = residual.shape[0]
+        row_count = routes.shape[1]
+        slot = lax.broadcasted_iota(jnp.int32, (SLOTS, row_count), 0)
+        place_of = lax.broadcasted_iota(jnp.int32, (SLOTS, row_count), 1)
+        expert = slot // 8
+        chosen = jnp.where(expert % 2 == 0, routes[0:1, :], routes[1:2, :])
+        picked = (chosen == expert) & (place_of // group_rows == owner)
+        before = lax.broadcasted_iota(jnp.int32, (row_count, row_count), 0)
+        after = lax.broadcasted_iota(jnp.int32, (row_count, row_count), 1)
+        upto = jnp.where(before <= after, 1.0, 0.0).astype(BF16)
+        rank = jnp.dot(
+            jnp.where(picked, 1.0, 0.0).astype(BF16), upto, preferred_element_type=F32
+        )
+        chosen_slot = picked & (rank == (slot % 8 + 1).astype(F32))
+        mine = lax.broadcasted_iota(jnp.int32, (group_rows, row_count), 1)
+        mine = mine == owner * group_rows + lax.broadcasted_iota(
+            jnp.int32, (group_rows, row_count), 0
+        )
+        mine_rows = jnp.where(mine, 1.0, 0.0).astype(BF16)
+
+        def across(left, right):
+            return lax.dot_general(
+                left, right, (((1,), (1,)), ((), ())), preferred_element_type=F32
+            ).astype(BF16)
+
+        pick[...] = across(jnp.where(chosen_slot, 1.0, 0.0).astype(BF16), mine_rows)
+        for column in range(2):
+            table = chosen_slot & (expert % 2 == column)
+            fetch[column] = across(mine_rows, jnp.where(table, 1.0, 0.0).astype(BF16))
+            share = jnp.sum(
+                jnp.where(mine, route_weights[column : column + 1, :], 0.0), axis=1, keepdims=True
+            )
+            shares[column] = jnp.broadcast_to(share, shares.shape[1:])
 
     loads = {}
 
@@ -466,10 +454,9 @@
             weights.append((kept, sent))
 
     def multiply_in(c):
-        for cc in (c, c + 1):
-            for h in range(2):
-                for copy in relay2[cc, h]:
-                    copy.wait_recv()
+        for h in range(2):
+            for copy in relay2[c, h]:
+                copy.wait_recv()
         if c == 0:
             for n in range(2):
                 weights[n][0].wait()
@@ -477,18 +464,17 @@
 
         def tile(t, carry):
             total = None
-            for cc in (c, c + 1):
-                for h in range(2):
-                    for sub in range(2):
-                        block = rows[cc, h, sub, pl.ds(2 * t, 2)].reshape(256, WIDTH)
-                        column = ((cc * 2 + h) * 2 + sub) * WIDTH
-                        term = lax.dot_general(
-                            w_in[:, column : column + WIDTH],
-                            block,
-                            (((1,), (1,)), ((), ())),
-                            preferred_element_type=F32,
-                        )
-                        total = term if total is None else total + term
+            for h in range(2):
+                for sub in range(2):
+                    block = rows[c, h, sub, pl.ds(2 * t, 2)].reshape(256, WIDTH)
+                    column = ((c * 2 + h) * 2 + sub) * WIDTH
+                    term = lax.dot_general(
+                        w_in[:, column : column + WIDTH],
+                        block,
+                        (((1,), (1,)), ((), ())),
+                        preferred_element_type=F32,
+                    )
+                    total = term if total is None else total + term
             pre[t] = total if c == 0 else pre[t] + total
             return carry
 
@@ -573,68 +559,83 @@
             produced = stacked(back, c, s).astype(BF16)
             for column in range(2):
                 fetched = jnp.dot(fetch[column], produced, preferred_element_type=F32)
-                value = value + shares[:, column : column + 1] * fetched
+                value = value + shares[column, :, 0:1] * fetched
             out[:, columns] = value.astype(BF16)
 
     load_proj(0)
     load_proj(1)
-    project(0)
-    pl.semaphore_wait(barrier, len(greeted))
-    send_proj(0)
-    scale_step = None
-    for tick in range(1, CHUNKS + 6):
-        if tick < CHUNKS:
-            project(tick)
-            send_proj(tick)
-        if tick == 2:
-            load_weights()
-        if 0 <= tick - 4 < CHUNKS:
-            gather_wide(tick - 4)
-        if 0 <= tick - 3 < CHUNKS:
-            gather_start(tick - 3)
-        if 0 <= tick - 1 < CHUNKS:
-            join_proj(tick - 1)
-        if 0 <= tick - 3 < CHUNKS:
-            gather_pass(tick - 3)
-        if 0 <= tick - 2 < CHUNKS:
-            dispatch(tick - 2)
-            if tick - 2 == CHUNKS - 1:
-                scale_step = send_scales()
-        if 0 <= tick - 5 < CHUNKS:
-            gather_wide_pass(tick - 5)
-        if tick - 2 == CHUNKS:
-            shared = share_scales(scale_step)
-        done = tick - 6
-        if 0 <= done < CHUNKS and done % 2 == 1 and done < CHUNKS - 1:
-            multiply_in(done - 1)
-    multiply_in(CHUNKS - 2)
+    residual_load = local(residual_hbm, residual)
+    tables()
+
+    def meet():
+        pl.semaphore_wait(barrier, size - 1 + len(column_peers))
+        load_weights()
+
+    attend(
+        meet, decay_exp, queries_hbm, keys_hbm, values_hbm, gates_hbm, attn_gain, settled,
+        queries, key_rows, value_rows, gate_rows, update, gathered, prior, state, inner,
+        state_sems, state_sems2, state_sems3, state_sems4, span_sems,
+    )
+    residual_load.wait()
+    for step, c in (
+        (project, 0), (send_proj, 0), (project, 1), (project, 2), (send_proj, 1),
+        (join_proj, 0), (join_proj, 1), (project, 3), (send_proj, 2), (project, 4),
+        (dispatch, 0), (dispatch, 1), (project, 5), (join_proj, 2), (send_proj, 3),
+        (gather_start, 0), (gather_start, 1), (gather_pass, 0), (dispatch, 2), (gather_pass, 1),
+        (send_proj, 4), (gather_wide, 0), (join_proj, 3), (gather_start, 2), (gather_wide, 1),
+        (send_proj, 5), (join_proj, 4), (dispatch, 3), (gather_pass, 2), (join_proj, 5),
+        (gather_wide_pass, 0), (gather_wide, 2), (gather_start, 3), (dispatch, 4),
+        (gather_wide_pass, 1), (dispatch, 5),
+    ):
+        step(c)
+    scale_step = send_scales()
+    for step, c in (
+        (gather_start, 4), (gather_pass, 3), (gather_wide_pass, 2), (gather_start, 5),
+        (gather_pass, 4),
+    ):
+        step(c)
+    shared = share_scales(scale_step)
+    for step, c in (
+        (gather_wide, 3), (multiply_in, 0), (gather_pass, 5), (gather_wide, 4),
+        (gather_wide, 5), (multiply_in, 1), (gather_wide_pass, 3), (multiply_in, 2),
+        (gather_wide_pass, 4), (gather_wide_pass, 5), (multiply_in, 3), (multiply_in, 4),
+        (multiply_in, 5),
+    ):
+        step(c)
     for copy in shared:
         copy.wait_recv()
     lax.fori_loop(0, 2, activate, 0)
     weights[2][0].wait()
     weights[2][1].wait_recv()
     copies.finish()
-    for step in range(CHUNKS + 6):
-        if step < CHUNKS:
-            multiply_out(step)
-            send_part(step)
-        if 0 <= step - 2 < CHUNKS:
-            join_part(step - 2)
-        if 0 <= step - 3 < CHUNKS:
-            send_mid(step - 3)
-        if 0 <= step - 4 < CHUNKS:
-            join_mid(step - 4)
-        if 0 <= step - 5 < CHUNKS:
-            send_home(step - 5)
-        if 0 <= step - 6 < CHUNKS:
-            finish(step - 6)
+    for step, c in (
+        (multiply_out, 0), (send_part, 0), (multiply_out, 1), (send_part, 1), (multiply_out, 2),
+        (send_part, 2), (multiply_out, 3), (join_part, 0), (multiply_out, 4), (multiply_out, 5),
+        (send_part, 3), (join_part, 1), (send_part, 4), (send_part, 5), (join_part, 2),
+        (join_part, 3), (join_part, 4), (join_part, 5), (send_mid, 0), (send_mid, 1),
+        (send_mid, 2), (send_mid, 3), (send_mid, 4), (join_mid, 0), (send_mid, 5),
+        (join_mid, 1), (join_mid, 2), (join_mid, 3), (join_mid, 4), (send_home, 0),
+        (join_mid, 5), (send_home, 1), (send_home, 2), (send_home, 3), (send_home, 4),
+        (send_home, 5), (finish, 0), (finish, 1), (finish, 2), (finish, 3), (finish, 4),
+        (finish, 5),
+    ):
+        step(c)
     copies.finish()
 
 
-def layer_tail(settled, out_proj, residual, norm_gain, pick, fetch, shares, w_gate, w_up, w_down):
+def layer(
+    queries, key_rows, value_rows, gate_rows, decay_exp, attn_gain, out_proj, residual,
+    norm_gain, routes, route_weights, w_gate, w_up, w_down,
+):
     units, width = w_gate.shape
     group_rows = residual.shape[0]
-    depth = settled.shape[1]
+    row_count, depth = queries.shape
+    head_count = decay_exp.shape[0]
+    head_width = depth // head_count
+    size = lax.axis_size("ctx")
+    states = pltpu.VMEM((size, head_count * head_width // size, head_width), BF16)
+    state_sems = pltpu.SemaphoreType.DMA((size - 1,))
+    span = pltpu.VMEM(queries.shape, BF16)
     half = 2 * WIDTH
     count = CHUNKS * (6 + 3 + 3 + 16 + 24) + 3 + 15 + 3
     whole = (CHUNKS, 2, 2, RING, RING, SLOTS, WIDTH)
@@ -644,9 +645,22 @@
     return pl.pallas_call(
         layer_kernel,
         out_shape=jax.ShapeDtypeStruct(residual.shape, BF16),
-        in_specs=[vmem, anywhere, vmem, vmem, vmem, vmem, vmem] + [anywhere] * 3,
+        in_specs=[pl.BlockSpec(memory_space=pltpu.SMEM)]
+        + [anywhere] * 4
+        + [vmem, anywhere, anywhere, vmem, vmem, vmem]
+        + [anywhere] * 3,
         out_specs=vmem,
-        scratch_shapes=[
+        scratch_shapes=[span] * 4
+        + [states] * 4
+        + [pltpu.VMEM((head_count, row_count, head_width), F32)]
+        + [state_sems] * 4
+        + [
+            pltpu.SemaphoreType.DMA((6,)),
+            span,
+            pltpu.VMEM(residual.shape, BF16),
+            pltpu.VMEM((SLOTS, group_rows), BF16),
+            pltpu.VMEM((2, group_rows, SLOTS), BF16),
+            pltpu.VMEM((2, group_rows, 128), F32),
             pltpu.VMEM((2, depth, 4 * WIDTH), BF16),
             pltpu.VMEM((CHUNKS, 2, RING, group_rows, half), BF16),
             pltpu.VMEM((CHUNKS, 6, group_rows, half), BF16),
@@ -672,14 +686,15 @@
             pltpu.VMEM(box, BF16),
             pltpu.SemaphoreType.DMA((count,)),
             pltpu.SemaphoreType.DMA((count,)),
-            pltpu.SemaphoreType.DMA((3 * CHUNKS + 4,)),
+            pltpu.SemaphoreType.DMA((3 * CHUNKS + 5,)),
         ],
         compiler_params=pltpu.CompilerParams(
             collective_id=2, has_side_effects=True, vmem_limit_bytes=64000 * 1024
         ),
-        name="layer_tail",
+        name="layer",
     )(
-        settled, out_proj, residual, norm_gain.reshape(1, width), pick, fetch, shares,
+        decay_exp, queries, key_rows, value_rows, gate_rows, attn_gain.reshape(1, depth),
+        out_proj, residual, norm_gain.reshape(1, width), routes.T, route_weights.T,
         w_gate, w_up, w_down,
     )
 
@@ -700,26 +715,18 @@
     w_up,
     w_down,
 ):
-    settled = attention(queries, key_rows, value_rows, gate_rows, decay_exp, attn_gain)
-    span_rows = queries.shape[0]
-    group_count = lax.axis_size("exp")
-    group_rows = span_rows // group_count
-    first_mine = lax.axis_index("exp") * group_rows
-    capacity = group_rows // 8
-    my_routes = lax.dynamic_slice_in_dim(routes, first_mine, group_rows, 0)
-    my_weights = lax.dynamic_slice_in_dim(route_weights, first_mine, group_rows, 0)
-    table = slot_table(my_routes, group_count, capacity)
-    pick = table.reshape(group_count * capacity, group_rows)
-    even = (jnp.arange(group_count * capacity) // capacity) % 2 == 0
-    fetch = jnp.stack([pick.T & even, pick.T & ~even]).astype(BF16)
-    return layer_tail(
-        settled,
+    return layer(
+        queries,
+        key_rows,
+        value_rows,
+        gate_rows,
+        decay_exp,
+        attn_gain,
         out_proj,
         residual,
         norm_gain,
-        pick.astype(BF16),
-        fetch,
-        my_weights,
+        routes,
+        route_weights,
         w_gate[0],
         w_up[0],
         w_down[0],

time: 163 us -> 132 us (0.81)
  Pallas kernels: 157 us -> 130 us
  local copies, waits for them, and re-layouts: 5.23 us -> 2.06 us
    pallas_call x2 -> x1, Pallas kernels: 157 us -> 130 us  [layer(): pl.pallas_call(layer_kernel, out_shape=jax.ShapeDtypeStruct(residual.shap...]
    unnamed x4 -> x1, local copies, waits for them, and re-layouts: 3.45 us -> 2.06 us
where the time goes in v5:
time: 132 us
  Pallas kernels  130 us (98%)
  local copies, waits for them, and re-layouts  2.06 us (2%)
    pallas_call x1, Pallas kernels, layer(): pl.pallas_call(layer_kernel, out_shape=jax.ShapeDtypeStruct(residual.shap...  130 us

profile of v5, /device:TPU:0, one launch (start us, length us, event | category | flops | bytes accessed | tf_op | source)
XLA Modules:
  0.0 132.0 jit_solution(17454982216661190308)
XLA Ops:
  0.0 129.9 %layer.1 = bf16[64,6144]{1,0:T(8,128)(2,1)} custom-call(s32[8]{0:T(128)} %decay_exp.1, bf16[256,1024]{1,0:T(8,128)(2,1)} %queries_hbm.1, bf16[256,1024]{1,0:T(8,128)(2,1)} %keys_hbm.1, bf16[256,1024]{1,0:T(8,128)(2,1)} %values_hbm.1, bf16[256,1024]{1,0:T(8,128)(2,1)} %gates_hbm.1, f32[1,1024]{1,0:T(1,128)} %bitcast.11, bf16[1024,6144]{1,0:T(8,128)(2,1)} %out_proj.1, ...), custom_call_target="tpu_custom_call" | custom-call | tf_op jit(solution)/shard_map/layer/pallas_call | solution.py:645
  129.9 2.1 %copy.16 = bf16[64,6144]{1,0:T(8,128)(2,1)} copy(bf16[64,6144]{1,0:T(8,128)(2,1)} %layer.1) | data formatting | bytes 1572864

commit v6 on v5

--- a/solution.py
+++ b/solution.py
@@ -17,7 +17,7 @@
 
 def attend(
     meet, decay_exp, queries_hbm, keys_hbm, values_hbm, gates_hbm, attn_gain, settled,
-    queries, key_rows, value_rows, gate_rows, update, gathered, prior, state, inner,
+    queries, key_rows, value_rows, gate_rows, update, gathered, prior, state, inner, factor,
     send_sems, recv_sems, send_sems2, recv_sems2, local_sems,
 ):
     index, owner = lax.axis_index("ctx"), lax.axis_index("exp")
@@ -112,6 +112,8 @@
         )
         mixing = (scores * damping).astype(BF16)
         inner[head] = jnp.dot(mixing, value_rows[:, columns(head)], preferred_element_type=F32)
+        gate = gate_rows[:, columns(head)].astype(F32)
+        factor[head] = attn_gain[:, columns(head)] / (1.0 + jnp.exp(-gate))
 
     loads[2].wait()
     loads[3].wait()
@@ -143,9 +145,7 @@
         mixed = inner[head] + reached * jnp.exp(-rate * (positions + 1.0))
         mean_square = jnp.mean(mixed * mixed, axis=1, keepdims=True)
         normed = mixed * lax.rsqrt(mean_square + EPSILON)
-        gate = gate_rows[:, columns(head)].astype(F32)
-        value = normed * attn_gain[:, columns(head)] * (1.0 / (1.0 + jnp.exp(-gate)))
-        settled[:, columns(head)] = value.astype(BF16)
+        settled[:, columns(head)] = (normed * factor[head]).astype(BF16)
     leave2()
 
 
@@ -181,11 +181,11 @@
 def layer_kernel(
     decay_exp, queries_hbm, keys_hbm, values_hbm, gates_hbm, attn_gain,
     out_proj, residual_hbm, norm_gain, routes, route_weights, w_gate, w_up, w_down, out,
-    queries, key_rows, value_rows, gate_rows, update, gathered, prior, state, inner,
+    queries, key_rows, value_rows, gate_rows, update, gathered, prior, state, inner, factor,
     state_sems, state_sems2, state_sems3, state_sems4, span_sems,
     settled, residual, pick, fetch, shares,
     proj_w, proj, in0, comb0, hidden, squares, outbox, inbox, scale_out, scale_in, scales,
-    rows, w_in, w_out, pre, act, in1, comb1, mid, in2, comb2, homebox, back,
+    rows, w_in, w_out, pre, act, in1, comb1, mid, in2, homebox, back,
     send_sems, recv_sems, local_sems,
 ):
     index, owner = lax.axis_index("ctx"), lax.axis_index("exp")
@@ -259,6 +259,25 @@
             ).astype(BF16)
             joined.append(copies.start(stage(sub), land(4 + sub), to))
         return joined
+
+    def scatter_direct(axis, view, land):
+        me, left, right, to_left, to_right, far = near[axis]
+        to_far = device(z, x_far) if axis == "x" else device(z_far, x)
+        return (
+            copies.start(view(0, far), land(4), to_far),
+            copies.start(view(1, far), land(5), to_far),
+            copies.start(view(0, right), land(2), to_right),
+            copies.start(view(1, left), land(3), to_left),
+            copies.start(view(0, left), land(0), to_left),
+            copies.start(view(1, right), land(1), to_right),
+        )
+
+    def total_direct(axis, view, land, sent, sub):
+        value = view(sub, near[axis][0])[...].astype(F32)
+        for n, i in ((4 + sub, sub), (2 + sub, 2 + sub), (sub, 4 + sub)):
+            sent[n].wait_recv()
+            value = value + land(i)[...].astype(F32)
+        return value
 
     def total(axis, view, land, sent, joined, sub):
         me = near[axis][0]
@@ -395,7 +414,7 @@
         scales[z, x] = jnp.broadcast_to(line, (8, 128))
         return [copies.start(scales.at[z, x], scales.at[z, x], other) for other in plane_peers]
 
-    gather1, relay1, gather2, relay2 = {}, {}, {}, {}
+    gather1, gather2, relay2 = {}, {}, {}
 
     def line_of(c, h, stage, sub, at):
         axis = (first if stage == 1 else second)[h]
@@ -406,7 +425,12 @@
     def spread(c, h, stage, started):
         me, left, right, to_left, to_right, far = near[(first if stage == 1 else second)[h]]
         mine = line_of(c, h, stage, both, me)
-        started[c, h] = (copies.start(mine, mine, to_right), copies.start(mine, mine, to_left))
+        sent = []
+        if stage == 1:
+            to_far = device(z, x_far) if first[h] == "x" else device(z_far, x)
+            sent = [copies.start(mine, mine, to_far)]
+        started[c, h] = [copies.start(mine, mine, to_right), copies.start(mine, mine, to_left)]
+        started[c, h] += sent
 
     def pass_on(c, h, stage, started, passed):
         me, left, right, to_left, to_right, far = near[(first if stage == 1 else second)[h]]
@@ -427,13 +451,9 @@
         for h in range(2):
             spread(c, h, 1, gather1)
 
-    def gather_pass(c):
-        for h in range(2):
-            pass_on(c, h, 1, gather1, relay1)
-
     def gather_wide(c):
         for h in range(2):
-            for copy in relay1[c, h]:
+            for copy in gather1[c, h]:
                 copy.wait_recv()
             spread(c, h, 2, gather2)
 
@@ -501,7 +521,7 @@
 
         lax.fori_loop(0, 4, block, 0)
 
-    sent1, joined1, sent2, joined2, returned = {}, {}, {}, {}, {}
+    sent1, joined1, sent2, returned = {}, {}, {}, {}
 
     def view1(c, h):
         if second[h] == "z":
@@ -533,18 +553,12 @@
                 mid[c, h, sub] = total(
                     second[h], view1(c, h), land1(c, h), sent1[c, h], joined1[c, h], sub
                 ).astype(BF16)
-            sent2[c, h] = scatter(first[h], view2(c, h), land2(c, h))
-
-    def join_mid(c):
-        for h in range(2):
-            joined2[c, h] = join(
-                first[h], view2(c, h), land2(c, h), lambda sub: comb2.at[c, h, sub], sent2[c, h]
-            )
+            sent2[c, h] = scatter_direct(first[h], view2(c, h), land2(c, h))
 
     def send_home(c):
         for h in range(2):
             for sub in range(2):
-                value = total(first[h], view2(c, h), land2(c, h), sent2[c, h], joined2[c, h], sub)
+                value = total_direct(first[h], view2(c, h), land2(c, h), sent2[c, h], sub)
                 for g in range(RING):
                     homebox[c, g, h, :, sub * WIDTH : (sub + 1) * WIDTH] = value[
                         8 * g : 8 * g + 8
@@ -573,7 +587,7 @@
 
     attend(
         meet, decay_exp, queries_hbm, keys_hbm, values_hbm, gates_hbm, attn_gain, settled,
-        queries, key_rows, value_rows, gate_rows, update, gathered, prior, state, inner,
+        queries, key_rows, value_rows, gate_rows, update, gathered, prior, state, inner, factor,
         state_sems, state_sems2, state_sems3, state_sems4, span_sems,
     )
     residual_load.wait()
@@ -581,25 +595,23 @@
         (project, 0), (send_proj, 0), (project, 1), (project, 2), (send_proj, 1),
         (join_proj, 0), (join_proj, 1), (project, 3), (send_proj, 2), (project, 4),
         (dispatch, 0), (dispatch, 1), (project, 5), (join_proj, 2), (send_proj, 3),
-        (gather_start, 0), (gather_start, 1), (gather_pass, 0), (dispatch, 2), (gather_pass, 1),
-        (send_proj, 4), (gather_wide, 0), (join_proj, 3), (gather_start, 2), (gather_wide, 1),
-        (send_proj, 5), (join_proj, 4), (dispatch, 3), (gather_pass, 2), (join_proj, 5),
-        (gather_wide_pass, 0), (gather_wide, 2), (gather_start, 3), (dispatch, 4),
-        (gather_wide_pass, 1), (dispatch, 5),
+        (gather_start, 0), (gather_start, 1), (dispatch, 2), (send_proj, 4), (gather_wide, 0),
+        (join_proj, 3), (gather_start, 2), (gather_wide, 1), (send_proj, 5), (join_proj, 4),
+        (dispatch, 3), (join_proj, 5), (gather_wide_pass, 0), (gather_wide, 2),
+        (gather_start, 3), (dispatch, 4), (gather_wide_pass, 1), (dispatch, 5),
     ):
         step(c)
     scale_step = send_scales()
     for step, c in (
-        (gather_start, 4), (gather_pass, 3), (gather_wide_pass, 2), (gather_start, 5),
-        (gather_pass, 4),
+        (gather_start, 4), (gather_wide_pass, 2), (gather_start, 5), (gather_wide, 3),
+        (multiply_in, 0),
     ):
         step(c)
     shared = share_scales(scale_step)
     for step, c in (
-        (gather_wide, 3), (multiply_in, 0), (gather_pass, 5), (gather_wide, 4),
-        (gather_wide, 5), (multiply_in, 1), (gather_wide_pass, 3), (multiply_in, 2),
-        (gather_wide_pass, 4), (gather_wide_pass, 5), (multiply_in, 3), (multiply_in, 4),
-        (multiply_in, 5),
+        (gather_wide, 4), (gather_wide, 5), (multiply_in, 1), (gather_wide_pass, 3),
+        (multiply_in, 2), (gather_wide_pass, 4), (gather_wide_pass, 5), (multiply_in, 3),
+        (multiply_in, 4), (multiply_in, 5),
     ):
         step(c)
     for copy in shared:
@@ -613,11 +625,9 @@
         (send_part, 2), (multiply_out, 3), (join_part, 0), (multiply_out, 4), (multiply_out, 5),
         (send_part, 3), (join_part, 1), (send_part, 4), (send_part, 5), (join_part, 2),
         (join_part, 3), (join_part, 4), (join_part, 5), (send_mid, 0), (send_mid, 1),
-        (send_mid, 2), (send_mid, 3), (send_mid, 4), (join_mid, 0), (send_mid, 5),
-        (join_mid, 1), (join_mid, 2), (join_mid, 3), (join_mid, 4), (send_home, 0),
-        (join_mid, 5), (send_home, 1), (send_home, 2), (send_home, 3), (send_home, 4),
-        (send_home, 5), (finish, 0), (finish, 1), (finish, 2), (finish, 3), (finish, 4),
-        (finish, 5),
+        (send_mid, 2), (send_mid, 3), (send_mid, 4), (send_mid, 5), (send_home, 0),
+        (send_home, 1), (send_home, 2), (send_home, 3), (send_home, 4), (send_home, 5),
+        (finish, 0), (finish, 1), (finish, 2), (finish, 3), (finish, 4), (finish, 5),
     ):
         step(c)
     copies.finish()
@@ -637,7 +647,7 @@
     state_sems = pltpu.SemaphoreType.DMA((size - 1,))
     span = pltpu.VMEM(queries.shape, BF16)
     half = 2 * WIDTH
-    count = CHUNKS * (6 + 3 + 3 + 16 + 24) + 3 + 15 + 3
+    count = CHUNKS * (6 + 3 + 3 + 14 + 24) + 3 + 15 + 3
     whole = (CHUNKS, 2, 2, RING, RING, SLOTS, WIDTH)
     box = (CHUNKS, RING, 2, SLOTS // RING, half)
     vmem = pl.BlockSpec(memory_space=pltpu.VMEM)
@@ -652,7 +662,7 @@
         out_specs=vmem,
         scratch_shapes=[span] * 4
         + [states] * 4
-        + [pltpu.VMEM((head_count, row_count, head_width), F32)]
+        + [pltpu.VMEM((head_count, row_count, head_width), F32)] * 2
         + [state_sems] * 4
         + [
             pltpu.SemaphoreType.DMA((6,)),
@@ -681,7 +691,6 @@
             pltpu.VMEM((CHUNKS, 2, 2, RING, SLOTS, WIDTH), BF16),
             pltpu.VMEM((CHUNKS, 2, 2, RING, SLOTS, WIDTH), BF16),
             pltpu.VMEM((CHUNKS, 2, 6, SLOTS, WIDTH), BF16),
-            pltpu.VMEM((CHUNKS, 2, 2, SLOTS, WIDTH), BF16),
             pltpu.VMEM(box, BF16),
             pltpu.VMEM(box, BF16),
             pltpu.SemaphoreType.DMA((count,)),

time: 132 us -> 130 us (0.985)
  Pallas kernels: 130 us -> 128 us
    pallas_call x1, Pallas kernels: 130 us -> 128 us  [layer(): pl.pallas_call(layer_kernel, out_shape=jax.ShapeDtypeStruct(residual.shap...]
where the time goes in v6:
time: 130 us
  Pallas kernels  128 us (98%)
  local copies, waits for them, and re-layouts  2.06 us (2%)
    pallas_call x1, Pallas kernels, layer(): pl.pallas_call(layer_kernel, out_shape=jax.ShapeDtypeStruct(residual.shap...  128 us

profile of v6, /device:TPU:0, one launch (start us, length us, event | category | flops | bytes accessed | tf_op | source)
XLA Modules:
  0.0 129.6 jit_solution(18036859823860064690)
XLA Ops:
  0.0 127.5 %layer.1 = bf16[64,6144]{1,0:T(8,128)(2,1)} custom-call(s32[8]{0:T(128)} %decay_exp.1, bf16[256,1024]{1,0:T(8,128)(2,1)} %queries_hbm.1, bf16[256,1024]{1,0:T(8,128)(2,1)} %keys_hbm.1, bf16[256,1024]{1,0:T(8,128)(2,1)} %values_hbm.1, bf16[256,1024]{1,0:T(8,128)(2,1)} %gates_hbm.1, f32[1,1024]{1,0:T(1,128)} %bitcast.11, bf16[1024,6144]{1,0:T(8,128)(2,1)} %out_proj.1, ...), custom_call_target="tpu_custom_call" | custom-call | tf_op jit(solution)/shard_map/layer/pallas_call | solution.py:655
  127.5 2.1 %copy.16 = bf16[64,6144]{1,0:T(8,128)(2,1)} copy(bf16[64,6144]{1,0:T(8,128)(2,1)} %layer.1) | data formatting | bytes 1572864

commit v7 on v6

--- a/solution.py
+++ b/solution.py
@@ -13,6 +13,7 @@
 CHUNKS = 6
 WIDTH = 256
 SLOTS = 32
+HEAD_PIECES = 3
 
 
 def attend(
@@ -414,7 +415,7 @@
         scales[z, x] = jnp.broadcast_to(line, (8, 128))
         return [copies.start(scales.at[z, x], scales.at[z, x], other) for other in plane_peers]
 
-    gather1, gather2, relay2 = {}, {}, {}
+    gather1, relay1, gather2, relay2 = {}, {}, {}, {}
 
     def line_of(c, h, stage, sub, at):
         axis = (first if stage == 1 else second)[h]
@@ -426,7 +427,7 @@
         me, left, right, to_left, to_right, far = near[(first if stage == 1 else second)[h]]
         mine = line_of(c, h, stage, both, me)
         sent = []
-        if stage == 1:
+        if stage == 1 and c < HEAD_PIECES:
             to_far = device(z, x_far) if first[h] == "x" else device(z_far, x)
             sent = [copies.start(mine, mine, to_far)]
         started[c, h] = [copies.start(mine, mine, to_right), copies.start(mine, mine, to_left)]
@@ -451,9 +452,15 @@
         for h in range(2):
             spread(c, h, 1, gather1)
 
+    def gather_pass(c):
+        if c < HEAD_PIECES:
+            return
+        for h in range(2):
+            pass_on(c, h, 1, gather1, relay1)
+
     def gather_wide(c):
         for h in range(2):
-            for copy in gather1[c, h]:
+            for copy in gather1[c, h] if c < HEAD_PIECES else relay1[c, h]:
                 copy.wait_recv()
             spread(c, h, 2, gather2)
 
@@ -595,23 +602,25 @@
         (project, 0), (send_proj, 0), (project, 1), (project, 2), (send_proj, 1),
         (join_proj, 0), (join_proj, 1), (project, 3), (send_proj, 2), (project, 4),
         (dispatch, 0), (dispatch, 1), (project, 5), (join_proj, 2), (send_proj, 3),
-        (gather_start, 0), (gather_start, 1), (dispatch, 2), (send_proj, 4), (gather_wide, 0),
-        (join_proj, 3), (gather_start, 2), (gather_wide, 1), (send_proj, 5), (join_proj, 4),
-        (dispatch, 3), (join_proj, 5), (gather_wide_pass, 0), (gather_wide, 2),
-        (gather_start, 3), (dispatch, 4), (gather_wide_pass, 1), (dispatch, 5),
+        (gather_start, 0), (gather_start, 1), (gather_pass, 0), (dispatch, 2), (gather_pass, 1),
+        (send_proj, 4), (gather_wide, 0), (join_proj, 3), (gather_start, 2), (gather_wide, 1),
+        (send_proj, 5), (join_proj, 4), (dispatch, 3), (gather_pass, 2), (join_proj, 5),
+        (gather_wide_pass, 0), (gather_wide, 2), (gather_start, 3), (dispatch, 4),
+        (gather_wide_pass, 1), (dispatch, 5),
     ):
         step(c)
     scale_step = send_scales()
     for step, c in (
-        (gather_start, 4), (gather_wide_pass, 2), (gather_start, 5), (gather_wide, 3),
-        (multiply_in, 0),
+        (gather_start, 4), (gather_pass, 3), (gather_wide_pass, 2), (gather_start, 5),
+        (gather_pass, 4),
     ):
         step(c)
     shared = share_scales(scale_step)
     for step, c in (
-        (gather_wide, 4), (gather_wide, 5), (multiply_in, 1), (gather_wide_pass, 3),
-        (multiply_in, 2), (gather_wide_pass, 4), (gather_wide_pass, 5), (multiply_in, 3),
-        (multiply_in, 4), (multiply_in, 5),
+        (gather_wide, 3), (multiply_in, 0), (gather_pass, 5), (gather_wide, 4),
+        (gather_wide, 5), (multiply_in, 1), (gather_wide_pass, 3), (multiply_in, 2),
+        (gather_wide_pass, 4), (gather_wide_pass, 5), (multiply_in, 3), (multiply_in, 4),
+        (multiply_in, 5),
     ):
         step(c)
     for copy in shared:
@@ -647,7 +656,7 @@
     state_sems = pltpu.SemaphoreType.DMA((size - 1,))
     span = pltpu.VMEM(queries.shape, BF16)
     half = 2 * WIDTH
-    count = CHUNKS * (6 + 3 + 3 + 14 + 24) + 3 + 15 + 3
+    count = CHUNKS * (6 + 3 + 3 + 16 + 24) + 3 + 15 + 3
     whole = (CHUNKS, 2, 2, RING, RING, SLOTS, WIDTH)
     box = (CHUNKS, RING, 2, SLOTS // RING, half)
     vmem = pl.BlockSpec(memory_space=pltpu.VMEM)

time: 130 us -> 129 us (level)
  no operation moved by 1% of the time
where the time goes in v7:
time: 129 us
  Pallas kernels  127 us (98%)
  local copies, waits for them, and re-layouts  2.06 us (2%)
    pallas_call x1, Pallas kernels, layer(): pl.pallas_call(layer_kernel, out_shape=jax.ShapeDtypeStruct(residual.shap...  127 us

profile of v7, /device:TPU:0, one launch (start us, length us, event | category | flops | bytes accessed | tf_op | source)
XLA Modules:
  0.0 129.0 jit_solution(12535667027921642765)
XLA Ops:
  0.0 126.9 %layer.1 = bf16[64,6144]{1,0:T(8,128)(2,1)} custom-call(s32[8]{0:T(128)} %decay_exp.1, bf16[256,1024]{1,0:T(8,128)(2,1)} %queries_hbm.1, bf16[256,1024]{1,0:T(8,128)(2,1)} %keys_hbm.1, bf16[256,1024]{1,0:T(8,128)(2,1)} %values_hbm.1, bf16[256,1024]{1,0:T(8,128)(2,1)} %gates_hbm.1, f32[1,1024]{1,0:T(1,128)} %bitcast.11, bf16[1024,6144]{1,0:T(8,128)(2,1)} %out_proj.1, ...), custom_call_target="tpu_custom_call" | custom-call | tf_op jit(solution)/shard_map/layer/pallas_call | solution.py:664
  126.9 2.1 %copy.16 = bf16[64,6144]{1,0:T(8,128)(2,1)} copy(bf16[64,6144]{1,0:T(8,128)(2,1)} %layer.1) | data formatting | bytes 1572864

commit v8 on v7

--- a/solution.py
+++ b/solution.py
@@ -526,7 +526,9 @@
             part[c, n // 2, n % 2] = value.astype(BF16).reshape(RING, RING, SLOTS, WIDTH)
             return carry
 
-        lax.fori_loop(0, 4, block, 0)
+        for h in range(2):
+            lax.fori_loop(2 * h, 2 * h + 2, block, 0)
+            sent1[c, h] = scatter(second[h], view1(c, h), land1(c, h))
 
     sent1, joined1, sent2, returned = {}, {}, {}, {}
 
@@ -543,10 +545,6 @@
 
     def land2(c, h):
         return lambda i: in2.at[c, h, i]
-
-    def send_part(c):
-        for h in range(2):
-            sent1[c, h] = scatter(second[h], view1(c, h), land1(c, h))
 
     def join_part(c):
         for h in range(2):
@@ -630,9 +628,9 @@
     weights[2][1].wait_recv()
     copies.finish()
     for step, c in (
-        (multiply_out, 0), (send_part, 0), (multiply_out, 1), (send_part, 1), (multiply_out, 2),
-        (send_part, 2), (multiply_out, 3), (join_part, 0), (multiply_out, 4), (multiply_out, 5),
-        (send_part, 3), (join_part, 1), (send_part, 4), (send_part, 5), (join_part, 2),
+        (multiply_out, 0), (multiply_out, 1), (multiply_out, 2),
+        (multiply_out, 3), (join_part, 0), (multiply_out, 4), (multiply_out, 5),
+        (join_part, 1), (join_part, 2),
         (join_part, 3), (join_part, 4), (join_part, 5), (send_mid, 0), (send_mid, 1),
         (send_mid, 2), (send_mid, 3), (send_mid, 4), (send_mid, 5), (send_home, 0),
         (send_home, 1), (send_home, 2), (send_home, 3), (send_home, 4), (send_home, 5),

time: 129 us -> 129 us (level)
  no operation moved by 1% of the time
where the time goes in v8:
time: 129 us
  Pallas kernels  127 us (98%)
  local copies, waits for them, and re-layouts  2.06 us (2%)
    pallas_call x1, Pallas kernels, layer(): pl.pallas_call(layer_kernel, out_shape=jax.ShapeDtypeStruct(residual.shap...  127 us

profile of v8, /device:TPU:0, one launch (start us, length us, event | category | flops | bytes accessed | tf_op | source)
XLA Modules:
  0.0 128.9 jit_solution(3533715821823135249)
XLA Ops:
  0.0 126.8 %layer.1 = bf16[64,6144]{1,0:T(8,128)(2,1)} custom-call(s32[8]{0:T(128)} %decay_exp.1, bf16[256,1024]{1,0:T(8,128)(2,1)} %queries_hbm.1, bf16[256,1024]{1,0:T(8,128)(2,1)} %keys_hbm.1, bf16[256,1024]{1,0:T(8,128)(2,1)} %values_hbm.1, bf16[256,1024]{1,0:T(8,128)(2,1)} %gates_hbm.1, f32[1,1024]{1,0:T(1,128)} %bitcast.11, bf16[1024,6144]{1,0:T(8,128)(2,1)} %out_proj.1, ...), custom_call_target="tpu_custom_call" | custom-call | tf_op jit(solution)/shard_map/layer/pallas_call | solution.py:662
  126.8 2.1 %copy.16 = bf16[64,6144]{1,0:T(8,128)(2,1)} copy(bf16[64,6144]{1,0:T(8,128)(2,1)} %layer.1) | data formatting | bytes 1572864
